TPU v7x, 32 devices: a whole 2x2x4 slice. The times are simulated.
32 devices in a mesh: dp: 8 (over z, x), expert: 4 (over y, core).
Axes of the slice: x: 2, y: 2, z: 4, core: 2. Of those that a mesh axis runs over, the one named last changes fastest.
Arguments:
- inputs: bfloat16 [32, 128, 2048], P(('dp', 'expert')), may hold values from -6 to 6
- cotangent: bfloat16 [32, 128, 2048], P(('dp', 'expert')), may hold values from -6 to 6
- lengths: int32 [32], P('dp'), may hold values from 1 to 128, 3072 in all
- dealing: int32 [8, 4], P('dp'), may hold values from 0 to 3, each once within a row
- routes: int32 [32, 128, 8], P(('dp', 'expert')), may hold values from 0 to 15, all different within a row; in each aligned block of 128 rows (0 to 127, 128 to 255, ..., all dimensions but the last counted through in order) at most 72 rows name the same one
- gate_values: float32 [32, 128, 8], P(('dp', 'expert')), may hold values from 0.25 to 0.75
- attn_gain: float32 [2048], replicated, may hold values from 0.1 to 1.9
- w_query: float32 [2048, 2048], P(('dp', 'expert')), may hold values from -0.125 to 0.125
- w_key: float32 [2048, 2048], P(('dp', 'expert')), may hold values from -0.125 to 0.125
- w_value: float32 [2048, 2048], P(('dp', 'expert')), may hold values from -0.125 to 0.125
- query_gain: float32 [2048], replicated, may hold values from 0.1 to 1.9
- key_gain: float32 [2048], replicated, may hold values from 0.1 to 1.9
- w_out: float32 [2048, 2048], P(('dp', 'expert')), may hold values from -0.5 to 0.5
- ffn_gain: float32 [2048], replicated, may hold values from 0.1 to 1.9
- w_gate: float32 [16, 2048, 1024], P('expert', 'dp'), may hold values from -0.125 to 0.125
- w_up: float32 [16, 2048, 1024], P('expert', 'dp'), may hold values from -0.125 to 0.125
- w_down: float32 [16, 1024, 2048], P('expert', 'dp'), may hold values from -0.1875 to 0.1875
Outputs:
- layer_out: bfloat16 [32, 128, 2048], P(('dp', 'expert'))
- grad_inputs: bfloat16 [32, 128, 2048], P(('dp', 'expert'))
- grad_attn_gain: float32 [2048], P(('dp', 'expert'))
- grad_w_query: float32 [2048, 2048], P(('dp', 'expert'))
- grad_w_key: float32 [2048, 2048], P(('dp', 'expert'))
- grad_w_value: float32 [2048, 2048], P(('dp', 'expert'))
- grad_query_gain: float32 [2048], P(('dp', 'expert'))
- grad_key_gain: float32 [2048], P(('dp', 'expert'))
- grad_w_out: float32 [2048, 2048], P(('dp', 'expert'))
- grad_ffn_gain: float32 [2048], P(('dp', 'expert'))
- grad_w_gate: float32 [16, 2048, 1024], P('expert', 'dp')
- grad_w_up: float32 [16, 2048, 1024], P('expert', 'dp')
- grad_w_down: float32 [16, 1024, 2048], P('expert', 'dp')
Inputs may be any that keep to these rules, and one draw needn't show every extreme that they name: `lengths`: the longest sequence has exactly 128 tokens. `dealing`: each row names every sequence of its group once. `routes`: each token names 8 different experts; within one dealt sequence no expert is named more than 72 times, and some sequence reaches 72 in every draw.
All inputs are finite; a program needn't handle non-finite values. No bound on the sum of `lengths` on one device may be relied on, other than what follows from the above.
Results may differ from a plain program's by a relative error of at most 0.015.
Values may be sent and summed in bfloat16 or wider, within the bound.
A program may use at most 384 MiB of HBM per device.

v0:
```python
import math

import jax
import jax.numpy as jnp
from jax import lax
from jax.sharding import PartitionSpec as P

HEADS = 16


epsilon = 1e-05


def norm_scale(values):
    return lax.rsqrt(jnp.mean(values * values, axis=-1, keepdims=True) + epsilon)


def norm_back(normed, row_scale, incoming):
    return row_scale * (incoming - normed * jnp.mean(incoming * normed, axis=-1, keepdims=True))


def angle_tables(length_rows, head_size):
    half_size = head_size // 2
    position = jnp.arange(length_rows, dtype=jnp.float32)[:, None]
    inverse = jnp.exp(
        jnp.arange(half_size, dtype=jnp.float32) * (-2.0 * math.log(10000.0) / head_size)
    )
    angles = position * inverse[None, :]
    return (jnp.cos(angles)[:, None, :], jnp.sin(angles)[:, None, :])


def rotate_pairs(values, cosine, sine_table):
    half_size = values.shape[-1] // 2
    first = values[..., :half_size]
    second = values[..., half_size:]
    return jnp.concatenate(
        [first * cosine - second * sine_table, second * cosine + first * sine_table], axis=-1
    )


def route_tables(expert_picks, experts, capacity):
    flat_picks = expert_picks.reshape(-1)
    onehot = (flat_picks[:, None] == jnp.arange(experts, dtype=jnp.int32)[None, :]).astype(
        jnp.int32
    )
    before = jnp.cumsum(onehot, axis=0) - onehot
    rank_within = jnp.sum(before * onehot, axis=1)
    slot_place = flat_picks * capacity + rank_within
    pair_count = flat_picks.shape[0]
    owner_pair = (
        jnp.zeros((experts * capacity,), jnp.int32)
        .at[slot_place]
        .set(jnp.arange(pair_count, dtype=jnp.int32))
    )
    filled = jnp.zeros((experts * capacity,), jnp.int32).at[slot_place].set(1)
    return (slot_place, owner_pair, filled)


def expert_front(received, gate_mat, up_mat):
    gate_pre = jnp.einsum("emd,edf->emf", received, gate_mat, preferred_element_type=jnp.float32)
    up_pre = jnp.einsum("emd,edf->emf", received, up_mat, preferred_element_type=jnp.float32)
    hidden_act = (jax.nn.silu(gate_pre) * up_pre).astype(jnp.bfloat16)
    return (gate_pre, up_pre, hidden_act)


def per_device(
    inputs,
    cotangent,
    lengths,
    dealing,
    routes,
    gate_values,
    attn_gain,
    w_query,
    w_key,
    w_value,
    query_gain,
    key_gain,
    w_out,
    ffn_gain,
    w_gate,
    w_up,
    w_down,
):
    group_size = lax.axis_size("expert")
    position = lax.axis_index("expert")
    deal_order = dealing[0]
    source = deal_order[position]
    dealt_rows = (
        lax.all_gather(inputs, "expert", axis=0, tiled=True),
        lax.all_gather(cotangent, "expert", axis=0, tiled=True),
    )
    seq_inputs = lax.dynamic_index_in_dim(dealt_rows[0], source, 0, keepdims=False).astype(
        jnp.float32
    )
    seq_grads = lax.dynamic_index_in_dim(dealt_rows[1], source, 0, keepdims=False).astype(
        jnp.float32
    )
    seq_length = lengths[source]
    length_rows, width = seq_inputs.shape
    head_size = width // HEADS
    attn_mats = (
        lax.all_gather(w_query.astype(jnp.bfloat16), ("dp", "expert"), axis=0, tiled=True),
        lax.all_gather(w_key.astype(jnp.bfloat16), ("dp", "expert"), axis=0, tiled=True),
        lax.all_gather(w_value.astype(jnp.bfloat16), ("dp", "expert"), axis=0, tiled=True),
        lax.all_gather(w_out.astype(jnp.bfloat16), ("dp", "expert"), axis=0, tiled=True),
    )
    query_mat, key_mat, value_mat, out_mat = attn_mats
    scale_in = norm_scale(seq_inputs)
    normed_in = seq_inputs * scale_in
    hidden_in = (normed_in * attn_gain).astype(jnp.bfloat16)
    query_raw = jnp.dot(hidden_in, query_mat, preferred_element_type=jnp.float32)
    key_raw = jnp.dot(hidden_in, key_mat, preferred_element_type=jnp.float32)
    values = jnp.dot(hidden_in, value_mat, preferred_element_type=jnp.float32).astype(jnp.bfloat16)
    cosine, sine_table = angle_tables(length_rows, head_size)
    query_scale = norm_scale(query_raw)
    query_normed = query_raw * query_scale
    key_scale = norm_scale(key_raw)
    key_normed = key_raw * key_scale
    queries = rotate_pairs(
        (query_normed * query_gain).reshape(length_rows, HEADS, head_size), cosine, sine_table
    ).astype(jnp.bfloat16)
    key_rows = rotate_pairs(
        (key_normed * key_gain).reshape(length_rows, HEADS, head_size), cosine, sine_table
    ).astype(jnp.bfloat16)
    head_values = values.reshape(length_rows, HEADS, head_size)
    factor = head_size ** (-0.5)
    row_index = jnp.arange(length_rows, dtype=jnp.int32)[:, None]
    col_index = jnp.arange(length_rows, dtype=jnp.int32)[None, :]
    visible = (col_index <= row_index) & (col_index < seq_length)
    scores = (
        jnp.einsum("ihd,jhd->hij", queries, key_rows, preferred_element_type=jnp.float32) * factor
    )
    scores = jnp.where(visible[None], scores, -1e30)
    weights = jax.nn.softmax(scores, axis=-1)
    weights_low = weights.astype(jnp.bfloat16)
    attended = jnp.einsum(
        "hij,jhd->ihd", weights_low, head_values, preferred_element_type=jnp.float32
    )
    attended = attended.reshape(length_rows, width).astype(jnp.bfloat16)
    residual = seq_inputs + jnp.dot(attended, out_mat, preferred_element_type=jnp.float32)
    scale_mid = norm_scale(residual)
    normed_mid = residual * scale_mid
    hidden_mid = (normed_mid * ffn_gain).astype(jnp.bfloat16)
    local_experts = w_gate.shape[0]
    experts = local_experts * group_size
    top_count = routes.shape[2]
    capacity = length_rows * top_count * 9 // (8 * experts)
    slot_place, owner_pair, filled = route_tables(routes[0], experts, capacity)
    live_slot = filled[:, None] > 0
    token_of_slot = owner_pair // top_count
    sending = jnp.where(live_slot, hidden_mid[token_of_slot], jnp.zeros((), jnp.bfloat16))
    sending = sending.reshape(group_size, local_experts, capacity, width)
    received = lax.all_to_all(sending, "expert", split_axis=0, concat_axis=2, tiled=True)[0]
    expert_mats = (
        lax.all_gather(w_gate.astype(jnp.bfloat16), "dp", axis=1, tiled=True),
        lax.all_gather(w_up.astype(jnp.bfloat16), "dp", axis=1, tiled=True),
        lax.all_gather(w_down.astype(jnp.bfloat16), "dp", axis=1, tiled=True),
    )
    gate_mat, up_mat, down_mat = expert_mats
    gate_pre, up_pre, hidden_act = expert_front(received, gate_mat, up_mat)
    expert_out = jnp.einsum(
        "emf,efd->emd", hidden_act, down_mat, preferred_element_type=jnp.float32
    ).astype(jnp.bfloat16)
    returned = lax.all_to_all(
        expert_out[None], "expert", split_axis=2, concat_axis=0, tiled=True
    ).reshape(experts * capacity, width)
    picked = returned[slot_place].reshape(length_rows, top_count, width)
    mixture = jnp.sum(gate_values[0][:, :, None] * picked.astype(jnp.float32), axis=1)
    layer_rows = (residual + mixture).astype(jnp.bfloat16)
    flat_gates = gate_values[0].reshape(-1)
    slot_grads = jnp.where(
        live_slot, flat_gates[owner_pair][:, None] * seq_grads[token_of_slot], 0.0
    ).astype(jnp.bfloat16)
    slot_grads = slot_grads.reshape(group_size, local_experts, capacity, width)
    out_grads = lax.all_to_all(slot_grads, "expert", split_axis=0, concat_axis=2, tiled=True)[0]
    gate_mat, up_mat, down_mat = (
        lax.all_gather(w_gate.astype(jnp.bfloat16), "dp", axis=1, tiled=True),
        lax.all_gather(w_up.astype(jnp.bfloat16), "dp", axis=1, tiled=True),
        lax.all_gather(w_down.astype(jnp.bfloat16), "dp", axis=1, tiled=True),
    )
    grad_hidden = jnp.einsum(
        "emd,efd->emf", out_grads, down_mat, preferred_element_type=jnp.float32
    )
    sigmoid_gate = jax.nn.sigmoid(gate_pre)
    grad_gate_pre = (
        grad_hidden * up_pre * sigmoid_gate * (1.0 + gate_pre * (1.0 - sigmoid_gate))
    ).astype(jnp.bfloat16)
    grad_up_pre = (grad_hidden * gate_pre * sigmoid_gate).astype(jnp.bfloat16)
    grad_slots = jnp.einsum(
        "emf,edf->emd", grad_gate_pre, gate_mat, preferred_element_type=jnp.float32
    )
    grad_slots = (
        grad_slots
        + jnp.einsum("emf,edf->emd", grad_up_pre, up_mat, preferred_element_type=jnp.float32)
    ).astype(jnp.bfloat16)
    grad_down = jnp.einsum(
        "emf,emd->efd", hidden_act, out_grads, preferred_element_type=jnp.float32
    )
    grad_gate = jnp.einsum(
        "emd,emf->edf", received, grad_gate_pre, preferred_element_type=jnp.float32
    )
    grad_up = jnp.einsum("emd,emf->edf", received, grad_up_pre, preferred_element_type=jnp.float32)
    expert_summed = (
        lax.psum_scatter(
            grad_gate.astype(jnp.bfloat16), "dp", scatter_dimension=1, tiled=True
        ).astype(jnp.float32),
        lax.psum_scatter(
            grad_up.astype(jnp.bfloat16), "dp", scatter_dimension=1, tiled=True
        ).astype(jnp.float32),
        lax.psum_scatter(
            grad_down.astype(jnp.bfloat16), "dp", scatter_dimension=1, tiled=True
        ).astype(jnp.float32),
    )
    sent_back = lax.all_to_all(
        grad_slots[None], "expert", split_axis=2, concat_axis=0, tiled=True
    ).reshape(experts * capacity, width)
    grad_mid = jnp.sum(
        sent_back[slot_place].reshape(length_rows, top_count, width).astype(jnp.float32), axis=1
    )
    ffn_gain_part = jnp.sum(grad_mid * normed_mid, axis=0)
    grad_resid = seq_grads + norm_back(normed_mid, scale_mid, grad_mid * ffn_gain)
    resid_low = grad_resid.astype(jnp.bfloat16)
    grad_out_mat = jnp.einsum("td,te->de", attended, resid_low, preferred_element_type=jnp.float32)
    grad_attended = jnp.einsum(
        "te,de->td", resid_low, out_mat, preferred_element_type=jnp.float32
    ).astype(jnp.bfloat16)
    grad_attended = grad_attended.reshape(length_rows, HEADS, head_size)
    grad_values = jnp.einsum(
        "hij,ihd->jhd", weights_low, grad_attended, preferred_element_type=jnp.float32
    )
    grad_values = grad_values.reshape(length_rows, width).astype(jnp.bfloat16)
    grad_weights = jnp.einsum(
        "ihd,jhd->hij", grad_attended, head_values, preferred_element_type=jnp.float32
    )
    grad_scores = (
        weights * (grad_weights - jnp.sum(weights * grad_weights, axis=-1, keepdims=True))
    ).astype(jnp.bfloat16)
    grad_queries = (
        jnp.einsum("hij,jhd->ihd", grad_scores, key_rows, preferred_element_type=jnp.float32)
        * factor
    )
    grad_keys = (
        jnp.einsum("hij,ihd->jhd", grad_scores, queries, preferred_element_type=jnp.float32)
        * factor
    )
    query_turned = rotate_pairs(grad_queries, cosine, -sine_table).reshape(length_rows, width)
    key_turned = rotate_pairs(grad_keys, cosine, -sine_table).reshape(length_rows, width)
    query_gain_part = jnp.sum(query_turned * query_normed, axis=0)
    key_gain_part = jnp.sum(key_turned * key_normed, axis=0)
    grad_query_raw = norm_back(query_normed, query_scale, query_turned * query_gain).astype(
        jnp.bfloat16
    )
    grad_key_raw = norm_back(key_normed, key_scale, key_turned * key_gain).astype(jnp.bfloat16)
    grad_query_mat = jnp.einsum(
        "td,te->de", hidden_in, grad_query_raw, preferred_element_type=jnp.float32
    )
    grad_key_mat = jnp.einsum(
        "td,te->de", hidden_in, grad_key_raw, preferred_element_type=jnp.float32
    )
    grad_value_mat = jnp.einsum(
        "td,te->de", hidden_in, grad_values, preferred_element_type=jnp.float32
    )
    grad_hidden_in = jnp.einsum(
        "te,de->td", grad_query_raw, query_mat, preferred_element_type=jnp.float32
    )
    grad_hidden_in = grad_hidden_in + jnp.einsum(
        "te,de->td", grad_key_raw, key_mat, preferred_element_type=jnp.float32
    )
    grad_hidden_in = grad_hidden_in + jnp.einsum(
        "te,de->td", grad_values, value_mat, preferred_element_type=jnp.float32
    )
    attn_gain_part = jnp.sum(grad_hidden_in * normed_in, axis=0)
    grad_seq = grad_resid + norm_back(normed_in, scale_in, grad_hidden_in * attn_gain)
    attn_summed = (
        lax.psum_scatter(grad_query_mat, ("dp", "expert"), scatter_dimension=0, tiled=True),
        lax.psum_scatter(grad_key_mat, ("dp", "expert"), scatter_dimension=0, tiled=True),
        lax.psum_scatter(grad_value_mat, ("dp", "expert"), scatter_dimension=0, tiled=True),
        lax.psum_scatter(grad_out_mat, ("dp", "expert"), scatter_dimension=0, tiled=True),
        lax.psum_scatter(attn_gain_part, ("dp", "expert"), scatter_dimension=0, tiled=True),
        lax.psum_scatter(query_gain_part, ("dp", "expert"), scatter_dimension=0, tiled=True),
        lax.psum_scatter(key_gain_part, ("dp", "expert"), scatter_dimension=0, tiled=True),
        lax.psum_scatter(ffn_gain_part, ("dp", "expert"), scatter_dimension=0, tiled=True),
    )
    back_rows = (
        lax.all_gather(layer_rows[None], "expert", axis=0, tiled=True),
        lax.all_gather(grad_seq.astype(jnp.bfloat16)[None], "expert", axis=0, tiled=True),
    )
    holder = jnp.sum(jnp.where(deal_order == position, jnp.arange(group_size, dtype=jnp.int32), 0))
    out_rows = lax.dynamic_slice_in_dim(back_rows[0], holder, 1, 0)
    grad_rows_out = lax.dynamic_slice_in_dim(back_rows[1], holder, 1, 0)
    return (
        out_rows,
        grad_rows_out,
        attn_summed[4],
        attn_summed[0],
        attn_summed[1],
        attn_summed[2],
        attn_summed[5],
        attn_summed[6],
        attn_summed[3],
        attn_summed[7],
        expert_summed[0],
        expert_summed[1],
        expert_summed[2],
    )


def solution(mesh):
    return jax.shard_map(
        per_device,
        mesh=mesh,
        in_specs=(
            P(("dp", "expert"), None, None),
            P(("dp", "expert"), None, None),
            P("dp"),
            P("dp", None),
            P(("dp", "expert"), None, None),
            P(("dp", "expert"), None, None),
            P(),
            P(("dp", "expert"), None),
            P(("dp", "expert"), None),
            P(("dp", "expert"), None),
            P(),
            P(),
            P(("dp", "expert"), None),
            P(),
            P("expert", "dp", None),
            P("expert", "dp", None),
            P("expert", "dp", None),
        ),
        out_specs=(
            P(("dp", "expert"), None, None),
            P(("dp", "expert"), None, None),
            P(("dp", "expert")),
            P(("dp", "expert"), None),
            P(("dp", "expert"), None),
            P(("dp", "expert"), None),
            P(("dp", "expert")),
            P(("dp", "expert")),
            P(("dp", "expert"), None),
            P(("dp", "expert")),
            P("expert", "dp", None),
            P("expert", "dp", None),
            P("expert", "dp", None),
        ),
        check_vma=False,
    )
```

profile of v0, /device:TPU:0, one launch (start us, length us, event | category | flops | bytes accessed | tf_op | source)
XLA Modules:
  0.0 2964.6 jit_solution(5224413650591121145)
XLA Ops:
  53.1 6.7 gather_fusion.3
  59.9 6.8 select_convert_fusion
  66.7 5.2 all-to-all-start.2
  73.3 84.0 %all-gather.20.cloned.1.call-done = bf16[2048,2048]{1,0:T(8,128)(2,1)} async-done(((bf16[64,2048]{1,0:T(8,128)(2,1)}), bf16[2048,2048]{1,0:T(8,128)(2,1)}) %all-gather.20.cloned.1.call-update) | async-done | bytes 8388624 | tf_op jit(solution)/shard_map/all_gather | solution.py:104
  163.5 73.0 %all-gather.18.cloned.1.call-done = bf16[2048,2048]{1,0:T(8,128)(2,1)} async-done(((bf16[64,2048]{1,0:T(8,128)(2,1)}), bf16[2048,2048]{1,0:T(8,128)(2,1)}) %all-gather.18.cloned.1.call-update) | async-done | bytes 8388624 | tf_op jit(solution)/shard_map/all_gather | solution.py:103
  249.2 66.8 %all-gather.16.cloned.1.call-done = bf16[2048,2048]{1,0:T(8,128)(2,1)} async-done(((bf16[64,2048]{1,0:T(8,128)(2,1)}), bf16[2048,2048]{1,0:T(8,128)(2,1)}) %all-gather.16.cloned.1.call-update) | async-done | bytes 8388624 | tf_op jit(solution)/shard_map/all_gather | solution.py:105
  316.0 5.5 fusion.14
  324.0 71.5 %all-gather.22.cloned.1.call-done = bf16[2048,2048]{1,0:T(8,128)(2,1)} async-done(((bf16[64,2048]{1,0:T(8,128)(2,1)}), bf16[2048,2048]{1,0:T(8,128)(2,1)}) %all-gather.22.cloned.1.call-update) | async-done | bytes 8388624 | tf_op jit(solution)/shard_map/all_gather | solution.py:106
  400.5 6.0 gather_fusion
  406.5 5.5 broadcast_select_fusion
  411.9 5.1 all-to-all-start
  417.1 5.4 copy.102
  422.4 48.5 %all-to-all-done = bf16[4,4,72,2048]{3,2,1,0:T(8,128)(2,1)} async-done(((bf16[4,4,72,2048]{3,2,1,0:T(8,128)(2,1)}), bf16[4,4,72,2048]{3,2,1,0:T(8,128)(2,1)}, u32[]{:S(2)}, u32[]{:S(2)}) %all-to-all-start) | async-done | bytes 4718624 | tf_op jit(solution)/shard_map/all_to_all | solution.py:154
  470.9 5.2 copy.98
  476.1 148.3 %all-gather.24.cloned.1.call-done = bf16[4,2048,1024]{2,1,0:T(8,128)(2,1)} async-done(((bf16[4,256,1024]{2,1,0:T(8,128)(2,1)}), bf16[4,2048,1024]{2,1,0:T(8,128)(2,1)}) %all-gather.24.cloned.1.call-update) | async-done | bytes 16777232 | tf_op jit(solution)/shard_map/all_gather | solution.py:156
  624.5 13.3 fusion.79
  637.7 215.3 %all-gather.26.cloned.1.call-done = bf16[4,2048,1024]{2,1,0:T(8,128)(2,1)} async-done(((bf16[4,256,1024]{2,1,0:T(8,128)(2,1)}), bf16[4,2048,1024]{2,1,0:T(8,128)(2,1)}) %all-gather.26.cloned.1.call-update) | async-done | bytes 16777232 | tf_op jit(solution)/shard_map/all_gather | solution.py:157
  853.0 13.2 fusion.80
  866.2 215.4 %all-gather.28.cloned.1.call-done = bf16[4,1024,2048]{2,1,0:T(8,128)(2,1)} async-done(((bf16[4,128,2048]{2,1,0:T(8,128)(2,1)}), bf16[4,1024,2048]{2,1,0:T(8,128)(2,1)}) %all-gather.28.cloned.1.call-update) | async-done | bytes 16777232 | tf_op jit(solution)/shard_map/all_gather | solution.py:158
  1081.6 15.1 multiply_convert_fusion
  1096.7 11.5 fusion.81
  1108.2 13.8 fusion.2
  1122.0 8.1 copy.103
  1135.3 11.5 convert_bitcast_fusion
  1146.7 5.8 copy.99
  1152.6 36.6 %all-to-all-done.3 = bf16[1,4,288,2048]{3,1,0,2:T(4,128)(2,1)} async-done(((bf16[1,4,288,2048]{3,1,0,2:T(4,128)(2,1)}), bf16[1,4,288,2048]{3,1,0,2:T(4,128)(2,1)}, u32[]{:S(2)}, u32[]{:S(2)}) %all-to-all-start.3) | async-done | bytes 4718624 | tf_op jit(solution)/shard_map/all_to_all | solution.py:215
  1194.3 7.2 copy.104
  1201.4 12.0 gather_fusion.4
  1218.8 29.2 all-to-all-done.1
  1247.9 7.1 copy.100
  1255.0 12.1 gather_fusion.1
  1267.2 6.5 fusion.1
  1276.0 7.2 convolution_convert_fusion.3
  1307.4 14.7 convolution_convert_fusion.2
  1322.2 15.2 convolution_convert_fusion.1
  1337.4 15.1 convolution_convert_fusion
  1352.6 9.2 fusion.37
  1363.0 8.2 fusion.28
  1372.2 8.3 fusion.67
  1381.5 8.3 fusion.69
  1393.1 42.3 %all-reduce.4 = (f32[2048]{0:T(1024)S(1)}, f32[2048]{0:T(1024)S(1)}, f32[2048]{0:T(1024)S(1)}, f32[2048]{0:T(1024)S(1)}) all-reduce(f32[2048]{0:T(1024)S(1)} %get-tuple-element.13, f32[2048]{0:T(1024)S(1)} %get-tuple-element.19, f32[2048]{0:T(1024)S(1)} %get-tuple-element.17, ...), channel_id=4, replica_groups=mesh['dp'=8,'expert'=4] {'dp','expert'}, use_global_device_ids=true, to_apply=%region_20.21.clone | all-reduce | flops 8192 | bytes 65536
  1441.5 197.3 %reduce-scatter.16.cloned.1.call-done = bf16[4,256,1024]{2,1,0:T(8,128)(2,1)} async-done(((bf16[4,2048,1024]{2,1,0:T(8,128)(2,1)}), bf16[4,256,1024]{2,1,0:T(8,128)(2,1)}) %reduce-scatter.16.cloned.1.call-update) | async-done | bytes 2097168 | tf_op jit(solution)/shard_map/reduce_scatter | solution.py:205
  1642.9 282.0 %reduce-scatter.18.cloned.1.call-done = bf16[4,256,1024]{2,1,0:T(8,128)(2,1)} async-done(((bf16[4,2048,1024]{2,1,0:T(8,128)(2,1)}), bf16[4,256,1024]{2,1,0:T(8,128)(2,1)}) %reduce-scatter.18.cloned.1.call-update) | async-done | bytes 2097168 | tf_op jit(solution)/shard_map/reduce_scatter | solution.py:208
  1928.9 281.2 %reduce-scatter.20.cloned.1.call-done = bf16[4,128,2048]{2,1,0:T(8,128)(2,1)} async-done(((bf16[4,1024,2048]{2,1,0:T(8,128)(2,1)}), bf16[4,128,2048]{2,1,0:T(8,128)(2,1)}) %reduce-scatter.20.cloned.1.call-update) | async-done | bytes 2097168 | tf_op jit(solution)/shard_map/reduce_scatter | solution.py:211
  2214.2 180.8 %reduce-scatter.14.cloned.1.call-done = f32[64,2048]{1,0:T(8,128)} async-done(((f32[2048,2048]{1,0:T(8,128)}), f32[64,2048]{1,0:T(8,128)}) %reduce-scatter.14.cloned.1.call-update) | async-done | bytes 524304 | tf_op jit(solution)/shard_map/reduce_scatter | solution.py:279
  2395.0 187.4 %reduce-scatter.12.cloned.1.call-done = f32[64,2048]{1,0:T(8,128)} async-done(((f32[2048,2048]{1,0:T(8,128)}), f32[64,2048]{1,0:T(8,128)}) %reduce-scatter.12.cloned.1.call-update) | async-done | bytes 524304 | tf_op jit(solution)/shard_map/reduce_scatter | solution.py:278
  2582.5 187.4 %reduce-scatter.10.cloned.1.call-done = f32[64,2048]{1,0:T(8,128)} async-done(((f32[2048,2048]{1,0:T(8,128)}), f32[64,2048]{1,0:T(8,128)}) %reduce-scatter.10.cloned.1.call-update) | async-done | bytes 524304 | tf_op jit(solution)/shard_map/reduce_scatter | solution.py:277
  2769.9 187.4 %reduce-scatter.8.cloned.1.call-done = f32[64,2048]{1,0:T(8,128)} async-done(((f32[2048,2048]{1,0:T(8,128)}), f32[64,2048]{1,0:T(8,128)}) %reduce-scatter.8.cloned.1.call-update) | async-done | bytes 524304 | tf_op jit(solution)/shard_map/reduce_scatter | solution.py:276
  (246 shorter events, 136.0 us)
Async XLA Ops:
  7.2 44.8 %all-gather.30.cloned.1.call-start = ((), (), s32[]{:S(2)}) async-start(), calls=%async_computation.19 | async-start | bytes 2621440 | tf_op jit(solution)/shard_map/all_gather | solution.py:91
  7.9 64.1 %all-gather.14.cloned.1.call-start = ((), (), s32[]{:S(2)}) async-start(), calls=%async_computation.11 | async-start | bytes 2621440 | tf_op jit(solution)/shard_map/all_gather | solution.py:90
  8.7 148.6 %all-gather.20.cloned.1.call-start = ((), (), s32[]{:S(2)}) async-start(), calls=%async_computation.14 | async-start | bytes 8650752 | tf_op jit(solution)/shard_map/all_gather | solution.py:104
  10.5 226.1 %all-gather.18.cloned.1.call-start = ((), (), s32[]{:S(2)}) async-start(), calls=%async_computation.13 | async-start | bytes 8650752 | tf_op jit(solution)/shard_map/all_gather | solution.py:103
  12.4 303.7 %all-gather.16.cloned.1.call-start = ((), (), s32[]{:S(2)}) async-start(), calls=%async_computation.12 | async-start | bytes 8650752 | tf_op jit(solution)/shard_map/all_gather | solution.py:105
  14.2 381.3 %all-gather.22.cloned.1.call-start = ((), (), s32[]{:S(2)}) async-start(), calls=%async_computation.15 | async-start | bytes 8650752 | tf_op jit(solution)/shard_map/all_gather | solution.py:106
  16.1 608.4 %all-gather.24.cloned.1.call-start = ((), (), s32[]{:S(2)}) async-start(), calls=%async_computation.16 | async-start | bytes 18874368 | tf_op jit(solution)/shard_map/all_gather | solution.py:156
  20.0 833.0 %all-gather.26.cloned.1.call-start = ((), (), s32[]{:S(2)}) async-start(), calls=%async_computation.17 | async-start | bytes 18874368 | tf_op jit(solution)/shard_map/all_gather | solution.py:157
  24.0 5.8 copy-start.34
  24.0 20.1 copy-start.32
  24.0 1057.6 %all-gather.28.cloned.1.call-start = ((), (), s32[]{:S(2)}) async-start(), calls=%async_computation.18 | async-start | bytes 18874368 | tf_op jit(solution)/shard_map/all_gather | solution.py:158
  30.1 19.6 copy-start.44
  35.4 16.6 copy-start.35
  51.1 270.4 %copy-start.37 = (pred[128,128]{0,1:T(8,128)(4,1)}, pred[128,128]{0,1:T(8,128)(4,1)S(1)}, u32[]{:S(2)}) copy-start(pred[128,128]{0,1:T(8,128)(4,1)S(1)} %fusion.48) | copy-start | bytes 49156
  52.0 191.4 %copy-start.22 = (f32[128,64]{1,0:T(8,128)}, f32[128,64]{1,0:T(8,128)S(1)}, u32[]{:S(2)}) copy-start(f32[128,64]{1,0:T(8,128)S(1)} %get-tuple-element.50) | copy-start | bytes 98308
  66.7 90.5 %copy-start.11 = (f32[2048]{0:T(1024)S(1)}, f32[2048]{0:T(1024)}, u32[]{:S(2)}) copy-start(f32[2048]{0:T(1024)} %param.23) | copy-start | bytes 24580
  66.7 345.2 %all-to-all-start.2 = ((bf16[4,4,72,2048]{3,2,1,0:T(8,128)(2,1)}), bf16[4,4,72,2048]{3,2,1,0:T(8,128)(2,1)}, u32[]{:S(2)}, u32[]{:S(2)}) async-start(bf16[4,4,72,2048]{3,2,1,0:T(8,128)(2,1)} %select_convert_fusion), calls=%async_computation.2 | async-start | bytes 9437184 | tf_op jit(solution)/shard_map/all_to_all | solution.py:176
  73.2 242.8 %copy-start.25 = (f32[128]{0:T(128)}, f32[128]{0:T(128)S(1)}, u32[]{:S(2)}) copy-start(f32[128]{0:T(128)S(1)} %add_rsqrt_fusion.3) | copy-start | bytes 1540
  73.2 89.9 %copy-start.28 = (f32[2048]{0:T(1024)S(1)}, f32[2048]{0:T(1024)}, u32[]{:S(2)}) copy-start(f32[2048]{0:T(1024)} %param.28) | copy-start | bytes 24580
  73.3 163.3 %copy-start.4 = (bf16[4,128,2048]{2,1,0:T(8,128)(2,1)S(1)}, bf16[4,128,2048]{2,1,0:T(8,128)(2,1)}, u32[]{:S(2)}) copy-start(bf16[4,128,2048]{2,1,0:T(8,128)(2,1)} %all-gather.14.cloned.1.call-done) | copy-start | bytes 6291460
  163.5 78.8 %copy-start.30 = (f32[2048]{0:T(1024)S(1)}, f32[2048]{0:T(1024)}, u32[]{:S(2)}) copy-start(f32[2048]{0:T(1024)} %param.27) | copy-start | bytes 24580
  245.7 75.8 %copy-start.13 = (bf16[128,16,64]{2,0,1:T(8,128)(2,1)}, bf16[128,16,64]{2,0,1:T(8,128)(2,1)S(1)}, u32[]{:S(2)}) copy-start(bf16[128,16,64]{2,0,1:T(8,128)(2,1)S(1)} %get-tuple-element.28) | copy-start | bytes 786436
  245.7 75.8 %copy-start.15 = (bf16[128,16,64]{2,0,1:T(8,128)(2,1)}, bf16[128,16,64]{2,0,1:T(8,128)(2,1)S(1)}, u32[]{:S(2)}) copy-start(bf16[128,16,64]{2,0,1:T(8,128)(2,1)S(1)} %get-tuple-element.29) | copy-start | bytes 786436
  249.2 72.3 %copy-start.38 = (f32[16,128]{1,0:T(8,128)}, f32[16,128]{1,0:T(8,128)S(1)}, u32[]{:S(2)}) copy-start(f32[16,128]{1,0:T(8,128)S(1)} %get-tuple-element.55) | copy-start | bytes 24580
  324.0 76.3 %copy-start.10 = (bf16[16,128,128]{2,1,0:T(8,128)(2,1)}, bf16[16,128,128]{2,1,0:T(8,128)(2,1)S(1)}, u32[]{:S(2)}) copy-start(bf16[16,128,128]{2,1,0:T(8,128)(2,1)S(1)} %convolution_convert_fusion.6) | copy-start | bytes 1572868
  395.5 4.8 copy-start.27
  411.9 59.0 %all-to-all-start = ((bf16[4,4,72,2048]{3,2,1,0:T(8,128)(2,1)}), bf16[4,4,72,2048]{3,2,1,0:T(8,128)(2,1)}, u32[]{:S(2)}, u32[]{:S(2)}) async-start(bf16[4,4,72,2048]{3,2,1,0:T(8,128)(2,1)} %broadcast_select_fusion), calls=%async_computation | async-start | bytes 9437184 | tf_op jit(solution)/shard_map/all_to_all | solution.py:154
  1130.1 59.0 %all-to-all-start.3 = ((bf16[1,4,288,2048]{3,1,0,2:T(4,128)(2,1)}), bf16[1,4,288,2048]{3,1,0,2:T(4,128)(2,1)}, u32[]{:S(2)}, u32[]{:S(2)}) async-start(bf16[1,4,288,2048]{3,1,0,2:T(4,128)(2,1)} %copy.103), calls=%async_computation.3 | async-start | bytes 9437184 | tf_op jit(solution)/shard_map/all_to_all | solution.py:215
  1152.6 41.6 %copy-start.33 = (f32[1,128,8]{1,2,0:T(8,128)S(1)}, f32[1,128,8]{1,2,0:T(8,128)}, u32[]{:S(2)}) copy-start(f32[1,128,8]{1,2,0:T(8,128)} %param.22) | copy-start | bytes 12292
  1152.6 41.7 %copy-start.36 = (s32[1024,1]{0,1:T(1,128)S(1)}, s32[1024,1]{0,1:T(1,128)}, u32[]{:S(2)}) copy-start(s32[1024,1]{0,1:T(1,128)} %copy-done.35) | copy-start | bytes 12292
  1189.1 58.8 %all-to-all-start.1 = ((bf16[1,4,288,2048]{3,1,0,2:T(4,128)(2,1)}), bf16[1,4,288,2048]{3,1,0,2:T(4,128)(2,1)}, u32[]{:S(2)}, u32[]{:S(2)}) async-start(bf16[1,4,288,2048]{3,1,0,2:T(4,128)(2,1)} %copy.99), calls=%async_computation.1 | async-start | bytes 9437184 | tf_op jit(solution)/shard_map/all_to_all | solution.py:165
  1194.1 243.7 %all-gather.34.cloned.1.call-start = ((), (), s32[]{:S(2)}) async-start(), calls=%async_computation.28 | async-start | bytes 2621440 | tf_op jit(solution)/shard_map/all_gather | solution.py:287
  1276.0 9.3 copy-start.14
  1276.0 9.3 copy-start.16
  1276.0 9.3 copy-start.17
  1276.0 9.3 copy-start.18
  1276.0 9.3 copy-start.39
  1293.7 5.5 copy-start.8
  1294.3 4.9 slice-start
  1296.3 5.9 slice-start.4
  1306.6 133.0 %all-gather.32.cloned.1.call-start = ((), (), s32[]{:S(2)}) async-start(), calls=%async_computation.27 | async-start | bytes 2621440 | tf_op jit(solution)/shard_map/all_gather | solution.py:286
  1307.3 331.4 %reduce-scatter.16.cloned.1.call-start = ((), (), s32[]{:S(2)}) async-start(), calls=%async_computation.24 | async-start | bytes 18874368 | tf_op jit(solution)/shard_map/reduce_scatter | solution.py:205
  1322.2 602.7 %reduce-scatter.18.cloned.1.call-start = ((), (), s32[]{:S(2)}) async-start(), calls=%async_computation.25 | async-start | bytes 18874368 | tf_op jit(solution)/shard_map/reduce_scatter | solution.py:208
  1337.4 872.7 %reduce-scatter.20.cloned.1.call-start = ((), (), s32[]{:S(2)}) async-start(), calls=%async_computation.26 | async-start | bytes 18874368 | tf_op jit(solution)/shard_map/reduce_scatter | solution.py:211
  1352.5 1042.5 %reduce-scatter.14.cloned.1.call-start = ((), (), s32[]{:S(2)}) async-start(), calls=%async_computation.23 | async-start | bytes 17301504 | tf_op jit(solution)/shard_map/reduce_scatter | solution.py:279
  1361.8 1220.7 %reduce-scatter.12.cloned.1.call-start = ((), (), s32[]{:S(2)}) async-start(), calls=%async_computation.22 | async-start | bytes 17301504 | tf_op jit(solution)/shard_map/reduce_scatter | solution.py:278
  1371.2 1398.7 %reduce-scatter.10.cloned.1.call-start = ((), (), s32[]{:S(2)}) async-start(), calls=%async_computation.21 | async-start | bytes 17301504 | tf_op jit(solution)/shard_map/reduce_scatter | solution.py:277
  1380.5 1576.8 %reduce-scatter.8.cloned.1.call-start = ((), (), s32[]{:S(2)}) async-start(), calls=%async_computation.20 | async-start | bytes 17301504 | tf_op jit(solution)/shard_map/reduce_scatter | solution.py:276
  (27 other events, 52.6 us)
Sparse Core Ops, SparseCore 0:
  9.6 25.2 all-gather.29
  36.5 22.6 all-gather.13
  62.6 94.6 all-gather.19
  160.5 76.0 all-gather.17
  239.8 76.1 all-gather.15
  319.3 76.1 all-gather.21
  398.2 226.1 all-gather.23
  627.2 225.7 all-gather.25
  855.8 225.7 all-gather.27
  1306.7 19.8 all-gather.33
  1328.8 22.5 all-gather.31
  1355.0 283.7 reduce-scatter.15
  1643.0 281.7 reduce-scatter.17
  1928.5 281.6 reduce-scatter.19
  2212.9 182.0 reduce-scatter.13
  2397.9 184.5 reduce-scatter.11
  2585.3 184.5 reduce-scatter.9
  2772.7 184.5 reduce-scatter.7
where the time goes:
time: 2970 us; the launch traced here: 2960 us
  waiting for transfers between devices  2490 us (84%)
  matrix products  205 us (7%)
  local copies, waits for them, and re-layouts  107 us (4%)
  other arithmetic  74.3 us (3%)
  blocking collectives  42.3 us (1%)
    reduce_scatter x1, waiting for transfers between devices, per_device(): lax.psum_scatter(grad_up.astype(jnp.bfloat16), 'dp', scatter_dimension=1,...  282 us
    reduce_scatter x1, waiting for transfers between devices, per_device(): lax.psum_scatter(grad_down.astype(jnp.bfloat16), 'dp', scatter_dimension=...  281 us
    all_gather x1, waiting for transfers between devices, per_device(): lax.all_gather(w_down.astype(jnp.bfloat16), 'dp', axis=1, tiled=True)  215 us
    all_gather x1, waiting for transfers between devices, per_device(): lax.all_gather(w_up.astype(jnp.bfloat16), 'dp', axis=1, tiled=True)  215 us
    reduce_scatter x1, waiting for transfers between devices, per_device(): lax.psum_scatter(grad_gate.astype(jnp.bfloat16), 'dp', scatter_dimension=...  197 us
    reduce_scatter x1, waiting for transfers between devices, per_device(): lax.psum_scatter(grad_value_mat, ('dp', 'expert'), scatter_dimension=0, t...  187 us
    reduce_scatter x1, waiting for transfers between devices, per_device(): lax.psum_scatter(grad_query_mat, ('dp', 'expert'), scatter_dimension=0, t...  187 us
    reduce_scatter x1, waiting for transfers between devices, per_device(): lax.psum_scatter(grad_key_mat, ('dp', 'expert'), scatter_dimension=0, til...  187 us
  transfers between devices with their start and end apart: 22, of which 17 were waited for; matrix products, arithmetic and copies ran while one was open for 9% of the time, Pallas kernels for 0%

commit v1 on v0

v1 whole, which is shorter than its diff:
```python
import math

import jax
import jax.numpy as jnp
from jax import lax
from jax.sharding import PartitionSpec as P

HEADS = 16


epsilon = 1e-05


def norm_scale(values):
    return lax.rsqrt(jnp.mean(values * values, axis=-1, keepdims=True) + epsilon)


def norm_back(normed, row_scale, incoming):
    return row_scale * (incoming - normed * jnp.mean(incoming * normed, axis=-1, keepdims=True))


def angle_tables(length_rows, head_size):
    half_size = head_size // 2
    position = jnp.arange(length_rows, dtype=jnp.float32)[:, None]
    inverse = jnp.exp(
        jnp.arange(half_size, dtype=jnp.float32) * (-2.0 * math.log(10000.0) / head_size)
    )
    angles = position * inverse[None, :]
    return (jnp.cos(angles)[:, None, :], jnp.sin(angles)[:, None, :])


def rotate_pairs(values, cosine, sine_table):
    half_size = values.shape[-1] // 2
    first = values[..., :half_size]
    second = values[..., half_size:]
    return jnp.concatenate(
        [first * cosine - second * sine_table, second * cosine + first * sine_table], axis=-1
    )


AXES = ("dp", "expert")


def expert_tables(routes, gates, expert, capacity):
    named = routes == expert
    member = jnp.any(named, axis=1)
    token_gate = jnp.sum(jnp.where(named, gates, 0.0), axis=1)
    tokens = member.shape[1]
    earlier = (
        jnp.arange(tokens, dtype=jnp.int32)[:, None] < jnp.arange(tokens, dtype=jnp.int32)[None, :]
    ).astype(jnp.float32)
    rank = jnp.dot(member.astype(jnp.float32), earlier, precision=lax.Precision.HIGHEST)
    place = jnp.where(member, rank.astype(jnp.int32), -1)
    hit = place[:, None, :] == jnp.arange(capacity, dtype=jnp.int32)[None, :, None]
    row_gate = jnp.sum(jnp.where(hit, token_gate[:, None, :], 0.0), axis=2)
    return hit, row_gate


def per_device(
    inputs,
    cotangent,
    lengths,
    dealing,
    routes,
    gate_values,
    attn_gain,
    w_query,
    w_key,
    w_value,
    query_gain,
    key_gain,
    w_out,
    ffn_gain,
    w_gate,
    w_up,
    w_down,
):
    low = jnp.bfloat16
    wide = jnp.float32
    group_size = lax.axis_size("expert")
    groups = lax.axis_size("dp")
    seqs = groups * group_size
    position = lax.axis_index("expert")
    group = lax.axis_index("dp")
    seq_inputs = inputs[0].astype(wide)
    seq_grads = cotangent[0].astype(wide)
    seq_length = lengths[position]
    length_rows, width = seq_inputs.shape
    head_size = width // HEADS
    top_count = routes.shape[2]
    local_experts, rows_held, hidden = w_gate.shape
    experts = local_experts * group_size
    capacity = length_rows * top_count * 9 // (8 * experts)
    shards = groups // local_experts
    expert = position * local_experts + group // shards
    block = hidden // groups
    hidden_part = hidden // shards

    payload = jnp.zeros((3 * top_count, length_rows), wide)
    payload = payload.at[:top_count].set(routes[0].T.astype(wide))
    payload = payload.at[top_count : 2 * top_count].set(gate_values[0].T)
    payload = payload.at[2 * top_count, :group_size].set(dealing[0].astype(wide))
    tables = lax.all_gather(payload, AXES, axis=0, tiled=False)
    deals = tables[:, 2 * top_count, :group_size].reshape(groups, group_size, group_size)[:, 0]
    deals = deals.astype(jnp.int32)
    slot_of = jnp.argmax(
        deals[:, None, :] == jnp.arange(group_size, dtype=jnp.int32)[None, :, None], axis=2
    )
    slot_of = (slot_of + jnp.arange(groups)[:, None] * group_size).reshape(-1)
    given = tables[slot_of]
    all_routes = given[:, :top_count].astype(jnp.int32)
    all_gates = given[:, top_count : 2 * top_count]
    hit, row_gate = expert_tables(all_routes, all_gates, expert, capacity)
    joined = 16 // math.gcd(16, capacity)
    bundles = seqs // joined
    eye = jnp.eye(joined, dtype=bool)
    select = (
        (hit.reshape(bundles, joined, capacity, 1, length_rows) & eye[None, :, None, :, None])
        .reshape(bundles, joined * capacity, joined * length_rows)
        .astype(low)
    )
    row_gate = row_gate.reshape(bundles, joined * capacity, 1)
    total_rows = seqs * capacity

    def to_owner(mat):
        mat = mat.astype(low).reshape(local_experts, rows_held, local_experts, shards, block)
        mat = mat.transpose(0, 3, 1, 2, 4).reshape(groups, rows_held, hidden_part)
        mat = lax.all_to_all(mat, "dp", split_axis=0, concat_axis=0, tiled=True)
        return mat.reshape(groups * rows_held, hidden_part)

    def to_master(grad):
        grad = grad.astype(low).reshape(groups, rows_held, hidden_part)
        grad = lax.all_to_all(grad, "dp", split_axis=0, concat_axis=0, tiled=True)
        grad = grad.reshape(local_experts, shards, rows_held, local_experts, block)
        return grad.transpose(0, 2, 3, 1, 4).reshape(local_experts, rows_held, hidden).astype(wide)

    same_shard = [
        [part + shards * index for index in range(local_experts)] for part in range(shards)
    ]

    def swap_down(mat):
        return lax.all_to_all(
            mat, "dp", split_axis=0, concat_axis=0, axis_index_groups=same_shard, tiled=True
        )

    gate_mat = to_owner(w_gate)
    up_mat = to_owner(w_up)
    down_mat = swap_down(w_down.astype(low)).reshape(hidden_part, width)

    attn_mats = (
        lax.all_gather(w_query.astype(low), AXES, axis=0, tiled=True),
        lax.all_gather(w_key.astype(low), AXES, axis=0, tiled=True),
        lax.all_gather(w_value.astype(low), AXES, axis=0, tiled=True),
        lax.all_gather(w_out.astype(low), AXES, axis=0, tiled=True),
    )
    query_mat, key_mat, value_mat, out_mat = attn_mats
    all_cotangent = lax.all_gather(cotangent, AXES, axis=0, tiled=True)
    scale_in = norm_scale(seq_inputs)
    normed_in = seq_inputs * scale_in
    hidden_in = (normed_in * attn_gain).astype(jnp.bfloat16)
    query_raw = jnp.dot(hidden_in, query_mat, preferred_element_type=jnp.float32)
    key_raw = jnp.dot(hidden_in, key_mat, preferred_element_type=jnp.float32)
    values = jnp.dot(hidden_in, value_mat, preferred_element_type=jnp.float32).astype(jnp.bfloat16)
    cosine, sine_table = angle_tables(length_rows, head_size)
    query_scale = norm_scale(query_raw)
    query_normed = query_raw * query_scale
    key_scale = norm_scale(key_raw)
    key_normed = key_raw * key_scale
    queries = rotate_pairs(
        (query_normed * query_gain).reshape(length_rows, HEADS, head_size), cosine, sine_table
    ).astype(jnp.bfloat16)
    key_rows = rotate_pairs(
        (key_normed * key_gain).reshape(length_rows, HEADS, head_size), cosine, sine_table
    ).astype(jnp.bfloat16)
    head_values = values.reshape(length_rows, HEADS, head_size)
    factor = head_size ** (-0.5)
    row_index = jnp.arange(length_rows, dtype=jnp.int32)[:, None]
    col_index = jnp.arange(length_rows, dtype=jnp.int32)[None, :]
    visible = (col_index <= row_index) & (col_index < seq_length)
    scores = (
        jnp.einsum("ihd,jhd->hij", queries, key_rows, preferred_element_type=jnp.float32) * factor
    )
    scores = jnp.where(visible[None], scores, -1e30)
    weights = jax.nn.softmax(scores, axis=-1)
    weights_low = weights.astype(jnp.bfloat16)
    attended = jnp.einsum(
        "hij,jhd->ihd", weights_low, head_values, preferred_element_type=jnp.float32
    )
    attended = attended.reshape(length_rows, width).astype(jnp.bfloat16)
    residual = seq_inputs + jnp.dot(attended, out_mat, preferred_element_type=jnp.float32)
    scale_mid = norm_scale(residual)
    normed_mid = residual * scale_mid
    hidden_mid = (normed_mid * ffn_gain).astype(jnp.bfloat16)
    all_hidden = lax.all_gather(hidden_mid[None], AXES, axis=0, tiled=True)
    bundled = all_hidden.reshape(bundles, joined * length_rows, width)
    rows = jnp.einsum("bct,btd->bcd", select, bundled, preferred_element_type=wide).astype(low)
    rows = rows.reshape(total_rows, width)
    bundled_grads = all_cotangent.reshape(bundles, joined * length_rows, width)
    out_grads = (
        row_gate
        * jnp.einsum("bct,btd->bcd", select, bundled_grads, preferred_element_type=wide)
    ).astype(low)
    out_grads = out_grads.reshape(total_rows, width)
    gate_pre = jnp.dot(rows, gate_mat, preferred_element_type=wide)
    up_pre = jnp.dot(rows, up_mat, preferred_element_type=wide)
    sigmoid_gate = jax.nn.sigmoid(gate_pre)
    hidden_act = (gate_pre * sigmoid_gate * up_pre).astype(low)
    expert_out = (
        row_gate
        * jnp.dot(hidden_act, down_mat, preferred_element_type=wide).reshape(
            bundles, joined * capacity, width
        )
    ).astype(low)
    out_part = jnp.einsum("bct,bcd->btd", select, expert_out, preferred_element_type=wide)
    out_part = out_part.astype(low).reshape(seqs, length_rows, width)
    grad_hidden = jnp.einsum("md,fd->mf", out_grads, down_mat, preferred_element_type=wide)
    grad_gate_pre = (
        grad_hidden * up_pre * sigmoid_gate * (1.0 + gate_pre * (1.0 - sigmoid_gate))
    ).astype(low)
    grad_up_pre = (grad_hidden * gate_pre * sigmoid_gate).astype(low)
    grad_slots = (
        jnp.einsum("mf,df->md", grad_gate_pre, gate_mat, preferred_element_type=wide)
        + jnp.einsum("mf,df->md", grad_up_pre, up_mat, preferred_element_type=wide)
    ).astype(low)
    mid_part = jnp.einsum(
        "bct,bcd->btd",
        select,
        grad_slots.reshape(bundles, joined * capacity, width),
        preferred_element_type=wide,
    )
    mid_part = mid_part.astype(low).reshape(seqs, length_rows, width)
    grad_mid = lax.psum_scatter(mid_part, AXES, scatter_dimension=0, tiled=True)[0].astype(wide)
    mixture = lax.psum_scatter(out_part, AXES, scatter_dimension=0, tiled=True)[0].astype(wide)
    layer_rows = (residual + mixture).astype(low)
    grad_down = jnp.einsum("mf,md->fd", hidden_act, out_grads, preferred_element_type=wide)
    grad_gate = jnp.einsum("md,mf->df", rows, grad_gate_pre, preferred_element_type=wide)
    grad_up = jnp.einsum("md,mf->df", rows, grad_up_pre, preferred_element_type=wide)
    expert_grads = (
        to_master(grad_gate),
        to_master(grad_up),
        swap_down(grad_down.astype(low).reshape(local_experts, block, width)).astype(wide),
    )
    ffn_gain_part = jnp.sum(grad_mid * normed_mid, axis=0)
    grad_resid = seq_grads + norm_back(normed_mid, scale_mid, grad_mid * ffn_gain)
    resid_low = grad_resid.astype(jnp.bfloat16)
    grad_out_mat = jnp.einsum("td,te->de", attended, resid_low, preferred_element_type=jnp.float32)
    grad_attended = jnp.einsum(
        "te,de->td", resid_low, out_mat, preferred_element_type=jnp.float32
    ).astype(jnp.bfloat16)
    grad_attended = grad_attended.reshape(length_rows, HEADS, head_size)
    grad_values = jnp.einsum(
        "hij,ihd->jhd", weights_low, grad_attended, preferred_element_type=jnp.float32
    )
    grad_values = grad_values.reshape(length_rows, width).astype(jnp.bfloat16)
    grad_weights = jnp.einsum(
        "ihd,jhd->hij", grad_attended, head_values, preferred_element_type=jnp.float32
    )
    grad_scores = (
        weights * (grad_weights - jnp.sum(weights * grad_weights, axis=-1, keepdims=True))
    ).astype(jnp.bfloat16)
    grad_queries = (
        jnp.einsum("hij,jhd->ihd", grad_scores, key_rows, preferred_element_type=jnp.float32)
        * factor
    )
    grad_keys = (
        jnp.einsum("hij,ihd->jhd", grad_scores, queries, preferred_element_type=jnp.float32)
        * factor
    )
    query_turned = rotate_pairs(grad_queries, cosine, -sine_table).reshape(length_rows, width)
    key_turned = rotate_pairs(grad_keys, cosine, -sine_table).reshape(length_rows, width)
    query_gain_part = jnp.sum(query_turned * query_normed, axis=0)
    key_gain_part = jnp.sum(key_turned * key_normed, axis=0)
    grad_query_raw = norm_back(query_normed, query_scale, query_turned * query_gain).astype(
        jnp.bfloat16
    )
    grad_key_raw = norm_back(key_normed, key_scale, key_turned * key_gain).astype(jnp.bfloat16)
    grad_query_mat = jnp.einsum(
        "td,te->de", hidden_in, grad_query_raw, preferred_element_type=jnp.float32
    )
    grad_key_mat = jnp.einsum(
        "td,te->de", hidden_in, grad_key_raw, preferred_element_type=jnp.float32
    )
    grad_value_mat = jnp.einsum(
        "td,te->de", hidden_in, grad_values, preferred_element_type=jnp.float32
    )
    grad_hidden_in = jnp.einsum(
        "te,de->td", grad_query_raw, query_mat, preferred_element_type=jnp.float32
    )
    grad_hidden_in = grad_hidden_in + jnp.einsum(
        "te,de->td", grad_key_raw, key_mat, preferred_element_type=jnp.float32
    )
    grad_hidden_in = grad_hidden_in + jnp.einsum(
        "te,de->td", grad_values, value_mat, preferred_element_type=jnp.float32
    )
    attn_gain_part = jnp.sum(grad_hidden_in * normed_in, axis=0)
    grad_seq = grad_resid + norm_back(normed_in, scale_in, grad_hidden_in * attn_gain)

    def to_rows(grad):
        return lax.psum_scatter(grad.astype(low), AXES, scatter_dimension=0, tiled=True).astype(wide)

    gain_parts = jnp.stack([attn_gain_part, query_gain_part, key_gain_part, ffn_gain_part])
    gains = lax.psum_scatter(gain_parts, AXES, scatter_dimension=1, tiled=True)
    return (
        layer_rows[None],
        grad_seq.astype(low)[None],
        gains[0],
        to_rows(grad_query_mat),
        to_rows(grad_key_mat),
        to_rows(grad_value_mat),
        gains[1],
        gains[2],
        to_rows(grad_out_mat),
        gains[3],
        *expert_grads,
    )


def solution(mesh):
    return jax.shard_map(
        per_device,
        mesh=mesh,
        in_specs=(
            P(("dp", "expert"), None, None),
            P(("dp", "expert"), None, None),
            P("dp"),
            P("dp", None),
            P(("dp", "expert"), None, None),
            P(("dp", "expert"), None, None),
            P(),
            P(("dp", "expert"), None),
            P(("dp", "expert"), None),
            P(("dp", "expert"), None),
            P(),
            P(),
            P(("dp", "expert"), None),
            P(),
            P("expert", "dp", None),
            P("expert", "dp", None),
            P("expert", "dp", None),
        ),
        out_specs=(
            P(("dp", "expert"), None, None),
            P(("dp", "expert"), None, None),
            P(("dp", "expert")),
            P(("dp", "expert"), None),
            P(("dp", "expert"), None),
            P(("dp", "expert"), None),
            P(("dp", "expert")),
            P(("dp", "expert")),
            P(("dp", "expert"), None),
            P(("dp", "expert")),
            P("expert", "dp", None),
            P("expert", "dp", None),
            P("expert", "dp", None),
        ),
        check_vma=False,
    )
```

time: 2970 us -> 1940 us (0.65)
  waiting for transfers between devices: 2490 us -> 1450 us
  blocking collectives: 42.3 us -> 108 us
  other arithmetic: 74.3 us -> 36.7 us
  local copies, waits for them, and re-layouts: 107 us -> 76.5 us
    reduce_scatter x7 -> x6, waiting for transfers between devices: 1500 us -> 880 us  [the longest x4 530 us: to_rows(): lax.psum_scatter(grad.astype(low), AXES, scatter_dimension=0, tiled=True)]
    all_gather x11 -> x6, waiting for transfers between devices: 874 us -> 379 us  [the longest x1 90 us: per_device(): all_hidden = lax.all_gather(hidden_mid[None], AXES, axis=0, tiled=True)]
    all_gather x0 -> x1, blocking collectives: none -> 108 us  [per_device(): tables = lax.all_gather(payload, AXES, axis=0, tiled=False)]
    all_to_all x4 -> x6, waiting for transfers between devices: 114 us -> 186 us  [the longest x2 73.5 us: to_master(): grad = lax.all_to_all(grad, 'dp', split_axis=0, concat_axis=0, tiled=True)]
    unnamed x1 -> x0, blocking collectives: 42.3 us -> none
    gather x5 -> x1, local copies, waits for them, and re-layouts: 41.4 us -> 0.59 us  [per_device(): given = tables[slot_of]]
    convert_element_type x0 -> x6, local copies, waits for them, and re-layouts: none -> 37.3 us  [to_master(): grad.transpose(0, 2, 3, 1, 4).reshape(local_experts, rows_held, hidden)]
    dot_general x9 -> x13, matrix products: 123 us -> 140 us  [the longest x1 24.5 us: per_device(): jnp.einsum('md,fd->mf', out_grads, down_mat, preferred_element_type=wide)]
  transfers between devices with their start and end apart: 22 -> 19, of which waited for: 17 -> 15; matrix products, arithmetic and copies ran while one was open for 9% -> 12% of each run, Pallas kernels for 0% -> 0%
where the time goes in v1:
time: 1940 us; the launch traced here: 1930 us
  waiting for transfers between devices  1450 us (75%)
  matrix products  212 us (11%)
  blocking collectives  108 us (6%)
  local copies, waits for them, and re-layouts  76.5 us (4%)
  starting transfers between devices  37.8 us (2%)
  other arithmetic  36.7 us (2%)
    reduce_scatter x4, waiting for transfers between devices, to_rows(): lax.psum_scatter(grad.astype(low), AXES, scatter_dimension=0, tiled=True)  530 us
    reduce_scatter x1, waiting for transfers between devices, per_device(): lax.psum_scatter(out_part, AXES, scatter_dimension=0, tiled=True)[0]  185 us
    reduce_scatter x1, waiting for transfers between devices, per_device(): lax.psum_scatter(mid_part, AXES, scatter_dimension=0, tiled=True)[0]  165 us
    all_gather x1, blocking collectives, per_device(): tables = lax.all_gather(payload, AXES, axis=0, tiled=False)  108 us
    all_gather x1, waiting for transfers between devices, per_device(): all_hidden = lax.all_gather(hidden_mid[None], AXES, axis=0, tiled=True)  90 us
    all_gather x1, waiting for transfers between devices, per_device(): lax.all_gather(w_key.astype(low), AXES, axis=0, tiled=True)  74 us
    all_to_all x2, waiting for transfers between devices, to_master(): grad = lax.all_to_all(grad, 'dp', split_axis=0, concat_axis=0, tiled=True)  73.5 us
    all_gather x1, waiting for transfers between devices, per_device(): lax.all_gather(w_query.astype(low), AXES, axis=0, tiled=True)  73.4 us
  transfers between devices with their start and end apart: 19, of which 15 were waited for; matrix products, arithmetic and copies ran while one was open for 12% of the time, Pallas kernels for 0%

profile of v1, /device:TPU:0, one launch (start us, length us, event | category | flops | bytes accessed | tf_op | source)
XLA Modules:
  0.0 1931.5 jit_solution(8590998739481783773)
XLA Ops:
  17.8 74.0 %all-gather.12.cloned.1.call-done = bf16[2048,2048]{1,0:T(8,128)(2,1)} async-done(((bf16[64,2048]{1,0:T(8,128)(2,1)}), bf16[2048,2048]{1,0:T(8,128)(2,1)}) %all-gather.12.cloned.1.call-update) | async-done | bytes 8388624 | tf_op jit(solution)/shard_map/all_gather | solution.py:152
  91.8 4.8 multiply_reduce_fusion.4
  98.0 73.4 %all-gather.10.cloned.1.call-done = bf16[2048,2048]{1,0:T(8,128)(2,1)} async-done(((bf16[64,2048]{1,0:T(8,128)(2,1)}), bf16[2048,2048]{1,0:T(8,128)(2,1)}) %all-gather.10.cloned.1.call-update) | async-done | bytes 8388624 | tf_op jit(solution)/shard_map/all_gather | solution.py:151
  171.4 4.8 multiply_reduce_fusion.5
  181.5 69.5 %all-gather.8.cloned.1.call-done = bf16[2048,2048]{1,0:T(8,128)(2,1)} async-done(((bf16[64,2048]{1,0:T(8,128)(2,1)}), bf16[2048,2048]{1,0:T(8,128)(2,1)}) %all-gather.8.cloned.1.call-update) | async-done | bytes 8388624 | tf_op jit(solution)/shard_map/all_gather | solution.py:153
  251.0 5.5 fusion.17
  258.7 71.8 %all-gather.14.cloned.1.call-done = bf16[2048,2048]{1,0:T(8,128)(2,1)} async-done(((bf16[64,2048]{1,0:T(8,128)(2,1)}), bf16[2048,2048]{1,0:T(8,128)(2,1)}) %all-gather.14.cloned.1.call-update) | async-done | bytes 8388624 | tf_op jit(solution)/shard_map/all_gather | solution.py:154
  330.5 4.8 multiply_reduce_fusion.3
  342.1 4.6 all-to-all-start
  351.6 71.7 %all-to-all-done = bf16[8,256,512]{1,2,0:T(8,128)(2,1)} async-done(((bf16[8,256,512]{1,2,0:T(8,128)(2,1)}), bf16[8,256,512]{1,2,0:T(8,128)(2,1)}, u32[]{:S(2)}, u32[]{:S(2)}) %all-to-all-start) | async-done | bytes 2097184 | tf_op jit(solution)/shard_map/all_to_all | solution.py:128
  427.5 108.2 %all_gather.32 = f32[32,24,128]{2,1,0:T(8,128)S(1)} all-gather(f32[1,24,128]{2,1,0:T(8,128)S(1)} %scatter.14), channel_id=1, replica_groups=mesh['dp'=8,'expert'=4] {'dp','expert'}, dimensions={0}, use_global_device_ids=true | all-gather | bytes 405504 | tf_op jit(solution)/shard_map/all_gather | solution.py:103
  552.9 14.9 all-to-all-start.2
  570.2 14.1 multiply_convert_fusion
  584.3 90.0 %all-gather.18.cloned.1.call-done = bf16[4096,2048]{1,0:T(8,128)(2,1)} async-done(((bf16[128,2048]{1,0:T(8,128)(2,1)}), bf16[4096,2048]{1,0:T(8,128)(2,1)}) %all-gather.18.cloned.1.call-update) | async-done | bytes 16777232 | tf_op jit(solution)/shard_map/all_gather | solution.py:194
  674.3 12.0 convolution_convert_fusion.6
  686.3 10.9 fusion.80
  697.3 6.7 fusion.79
  704.0 24.5 %multiply_convert_fusion.3 = (bf16[2304,512]{1,0:T(8,128)(2,1)}, bf16[2304,512]{1,0:T(8,128)(2,1)S(1)}, bf16[2304,512]{1,0:T(8,128)(2,1)}) fusion(f32[2304,512]{1,0:T(8,128)} %fusion.79, f32[2304,512]{1,0:T(8,128)} %fusion.80, bf16[2304,2048]{1,0:T(8,128)(2,1)} %bitcast.232, bf16[512,2048]{1,0:T(8,128)(2,1)} %bitcast.25), kind=kOutput, calls=%fused_computation.14 | convolution fusion | flops 4850712576 | bytes 28049408 | tf_op jit(solution)/shard_map/md,fd->mf/dot_general | solution.py:216
  728.4 9.1 fusion.81
  737.6 10.3 add_convert_fusion
  747.9 9.3 convolution_convert_fusion
  759.1 14.3 convolution_convert_fusion.1
  773.8 164.7 %reduce-scatter.12.cloned.1.call-done = bf16[1,128,2048]{2,1,0:T(8,128)(2,1)} async-done(((bf16[32,128,2048]{2,1,0:T(8,128)(2,1)}), bf16[1,128,2048]{2,1,0:T(8,128)(2,1)}) %reduce-scatter.12.cloned.1.call-update) | async-done | bytes 524304 | tf_op jit(solution)/shard_map/reduce_scatter | solution.py:232
  940.0 185.4 %reduce-scatter.10.cloned.1.call-done = bf16[1,128,2048]{2,1,0:T(8,128)(2,1)} async-done(((bf16[32,128,2048]{2,1,0:T(8,128)(2,1)}), bf16[1,128,2048]{2,1,0:T(8,128)(2,1)}) %reduce-scatter.10.cloned.1.call-update) | async-done | bytes 524304 | tf_op jit(solution)/shard_map/reduce_scatter | solution.py:233
  1127.9 7.2 convolution_convert_fusion.10
  1151.5 4.4 convolution_add_fusion.1
  1161.6 5.6 convolution_convert_fusion.2
  1168.2 5.7 convolution_convert_fusion.3
  1174.0 5.7 convolution_convert_fusion.4
  1180.0 5.7 convolution_convert_fusion.5
  1185.8 9.4 convolution_convert_fusion.7
  1195.2 4.4 all-to-all-start.5
  1199.6 9.4 convolution_convert_fusion.9
  1209.0 40.6 %all-to-all-done.5 = bf16[4,128,2048]{2,1,0:T(8,128)(2,1)} async-done(((bf16[4,128,2048]{2,1,0:T(8,128)(2,1)}), bf16[4,128,2048]{2,1,0:T(8,128)(2,1)}, u32[]{:S(2)}, u32[]{:S(2)}) %all-to-all-start.5) | async-done | bytes 2097184 | tf_op jit(solution)/shard_map/all_to_all | solution.py:142
  1254.0 9.3 convolution_convert_fusion.8
  1263.3 41.7 %all-to-all-done.3 = bf16[8,256,512]{2,1,0:T(8,128)(2,1)} async-done(((bf16[8,256,512]{2,1,0:T(8,128)(2,1)}), bf16[8,256,512]{2,1,0:T(8,128)(2,1)}, u32[]{:S(2)}, u32[]{:S(2)}) %all-to-all-start.3) | async-done | bytes 2097184 | tf_op jit(solution)/shard_map/all_to_all | solution.py:133
  1305.0 4.6 all-to-all-start.4
  1313.7 4.7 reshape.455
  1318.5 7.5 copy.213
  1325.9 6.4 reshape.453
  1332.3 31.8 %all-to-all-done.4 = bf16[8,256,512]{2,1,0:T(8,128)(2,1)} async-done(((bf16[8,256,512]{2,1,0:T(8,128)(2,1)}), bf16[8,256,512]{2,1,0:T(8,128)(2,1)}, u32[]{:S(2)}, u32[]{:S(2)}) %all-to-all-start.4) | async-done | bytes 2097184 | tf_op jit(solution)/shard_map/all_to_all | solution.py:133
  1364.2 4.7 reshape.456
  1368.9 7.5 copy.212
  1376.4 6.5 reshape.454
  1387.4 94.4 %reduce-scatter.20.cloned.1.call-done = bf16[64,2048]{1,0:T(8,128)(2,1)} async-done(((bf16[2048,2048]{1,0:T(8,128)(2,1)}), bf16[64,2048]{1,0:T(8,128)(2,1)}) %reduce-scatter.20.cloned.1.call-update) | async-done | bytes 262160 | tf_op jit(solution)/shard_map/reduce_scatter | solution.py:299
  1483.5 145.3 %reduce-scatter.18.cloned.1.call-done = bf16[64,2048]{1,0:T(8,128)(2,1)} async-done(((bf16[2048,2048]{1,0:T(8,128)(2,1)}), bf16[64,2048]{1,0:T(8,128)(2,1)}) %reduce-scatter.18.cloned.1.call-update) | async-done | bytes 262160 | tf_op jit(solution)/shard_map/reduce_scatter | solution.py:299
  1630.6 145.1 %reduce-scatter.16.cloned.1.call-done = bf16[64,2048]{1,0:T(8,128)(2,1)} async-done(((bf16[2048,2048]{1,0:T(8,128)(2,1)}), bf16[64,2048]{1,0:T(8,128)(2,1)}) %reduce-scatter.16.cloned.1.call-update) | async-done | bytes 262160 | tf_op jit(solution)/shard_map/reduce_scatter | solution.py:299
  1777.5 145.3 %reduce-scatter.14.cloned.1.call-done = bf16[64,2048]{1,0:T(8,128)(2,1)} async-done(((bf16[2048,2048]{1,0:T(8,128)(2,1)}), bf16[64,2048]{1,0:T(8,128)(2,1)}) %reduce-scatter.14.cloned.1.call-update) | async-done | bytes 262160 | tf_op jit(solution)/shard_map/reduce_scatter | solution.py:299
  (235 shorter events, 103.9 us)
Async XLA Ops:
  7.2 8.1 copy-start.45
  7.2 9.4 copy-start
  7.2 84.6 %copy-start.14 = (f32[2048]{0:T(1024)S(1)}, f32[2048]{0:T(1024)}, u32[]{:S(2)}) copy-start(f32[2048]{0:T(1024)} %param.29) | copy-start | bytes 24580
  7.2 84.6 %all-gather.12.cloned.1.call-start = ((), (), s32[]{:S(2)}) async-start(), calls=%async_computation.15 | async-start | bytes 8650752 | tf_op jit(solution)/shard_map/all_gather | solution.py:152
  9.1 162.3 %all-gather.10.cloned.1.call-start = ((), (), s32[]{:S(2)}) async-start(), calls=%async_computation.14 | async-start | bytes 8650752 | tf_op jit(solution)/shard_map/all_gather | solution.py:151
  11.0 240.1 %all-gather.8.cloned.1.call-start = ((), (), s32[]{:S(2)}) async-start(), calls=%async_computation.13 | async-start | bytes 8650752 | tf_op jit(solution)/shard_map/all_gather | solution.py:153
  12.8 317.7 %all-gather.14.cloned.1.call-start = ((), (), s32[]{:S(2)}) async-start(), calls=%async_computation.16 | async-start | bytes 8650752 | tf_op jit(solution)/shard_map/all_gather | solution.py:154
  14.6 555.5 %all-gather.16.cloned.1.call-start = ((), (), s32[]{:S(2)}) async-start(), calls=%async_computation.18 | async-start | bytes 17301504 | tf_op jit(solution)/shard_map/all_gather | solution.py:157
  15.2 659.1 %all-gather.18.cloned.1.call-start = ((), (), s32[]{:S(2)}) async-start(), calls=%async_computation.24 | async-start | bytes 17301504 | tf_op jit(solution)/shard_map/all_gather | solution.py:194
  16.8 234.3 %copy-start.32 = (f32[128]{0:T(128)}, f32[128]{0:T(128)S(1)}, u32[]{:S(2)}) copy-start(f32[128]{0:T(128)S(1)} %add_rsqrt_fusion.3) | copy-start | bytes 1540
  17.7 160.5 %copy-start.29 = (f32[128,64]{1,0:T(8,128)}, f32[128,64]{1,0:T(8,128)S(1)}, u32[]{:S(2)}) copy-start(f32[128,64]{1,0:T(8,128)S(1)} %get-tuple-element.88) | copy-start | bytes 98308
  17.8 79.8 %copy-start.35 = (f32[2048]{0:T(1024)S(1)}, f32[2048]{0:T(1024)}, u32[]{:S(2)}) copy-start(f32[2048]{0:T(1024)} %param.34) | copy-start | bytes 24580
  97.9 79.2 %copy-start.37 = (f32[2048]{0:T(1024)S(1)}, f32[2048]{0:T(1024)}, u32[]{:S(2)}) copy-start(f32[2048]{0:T(1024)} %param.33) | copy-start | bytes 24580
  179.6 76.9 %copy-start.16 = (bf16[128,16,64]{2,0,1:T(8,128)(2,1)}, bf16[128,16,64]{2,0,1:T(8,128)(2,1)S(1)}, u32[]{:S(2)}) copy-start(bf16[128,16,64]{2,0,1:T(8,128)(2,1)S(1)} %get-tuple-element.80) | copy-start | bytes 786436
  179.6 76.9 %copy-start.18 = (bf16[128,16,64]{2,0,1:T(8,128)(2,1)}, bf16[128,16,64]{2,0,1:T(8,128)(2,1)S(1)}, u32[]{:S(2)}) copy-start(bf16[128,16,64]{2,0,1:T(8,128)(2,1)S(1)} %get-tuple-element.81) | copy-start | bytes 786436
  179.6 76.9 %copy-start.20 = (bf16[128,16,64]{2,0,1:T(8,128)(2,1)}, bf16[128,16,64]{2,0,1:T(8,128)(2,1)S(1)}, u32[]{:S(2)}) copy-start(bf16[128,16,64]{2,0,1:T(8,128)(2,1)S(1)} %get-tuple-element.64) | copy-start | bytes 786436
  179.6 76.9 %copy-start.22 = (bf16[128,16,64]{2,0,1:T(8,128)(2,1)}, bf16[128,16,64]{2,0,1:T(8,128)(2,1)S(1)}, u32[]{:S(2)}) copy-start(bf16[128,16,64]{2,0,1:T(8,128)(2,1)S(1)} %get-tuple-element.65) | copy-start | bytes 786436
  258.6 76.6 %copy-start.11 = (bf16[16,128,128]{2,1,0:T(8,128)(2,1)}, bf16[16,128,128]{2,1,0:T(8,128)(2,1)S(1)}, u32[]{:S(2)}) copy-start(bf16[16,128,128]{2,1,0:T(8,128)(2,1)S(1)} %convolution_convert_fusion.13) | copy-start | bytes 1572868
  330.5 5.7 copy-start.34
  342.1 81.2 %all-to-all-start = ((bf16[8,256,512]{1,2,0:T(8,128)(2,1)}), bf16[8,256,512]{1,2,0:T(8,128)(2,1)}, u32[]{:S(2)}, u32[]{:S(2)}) async-start(bf16[8,256,512]{1,2,0:T(8,128)(2,1)} %bitcast.243), calls=%async_computation | async-start | bytes 4194304 | tf_op jit(solution)/shard_map/all_to_all | solution.py:128
  350.1 77.2 %copy-start.43 = (s32[1,128,8]{1,2,0:T(8,128)S(1)}, s32[1,128,8]{1,2,0:T(8,128)}, u32[]{:S(2)}) copy-start(s32[1,128,8]{1,2,0:T(8,128)} %param.27) | copy-start | bytes 12292
  350.1 77.2 %copy-start.46 = (s32[1,4]{1,0:T(1,128)S(1)}, s32[1,4]{1,0:T(1,128)}, u32[]{:S(2)}) copy-start(s32[1,4]{1,0:T(1,128)} %param.26) | copy-start | bytes 52
  350.1 77.2 %copy-start.44 = (f32[1,128,8]{1,2,0:T(8,128)S(1)}, f32[1,128,8]{1,2,0:T(8,128)}, u32[]{:S(2)}) copy-start(f32[1,128,8]{1,2,0:T(8,128)} %param.28) | copy-start | bytes 12292
  423.3 129.6 %all-to-all-start.1 = ((bf16[8,256,512]{1,2,0:T(8,128)(2,1)}), bf16[8,256,512]{1,2,0:T(8,128)(2,1)S(1)}, u32[]{:S(2)}, u32[]{:S(2)}) async-start(bf16[8,256,512]{1,2,0:T(8,128)(2,1)} %bitcast.242), calls=%async_computation.1 | async-start | bytes 4194304 | tf_op jit(solution)/shard_map/all_to_all | solution.py:128
  544.9 129.5 %copy-start.3 = (pred[16,144,256]{2,1,0:T(8,128)(4,1)}, pred[16,144,256]{2,1,0:T(8,128)(4,1)S(1)}, u32[]{:S(2)}) copy-start(pred[16,144,256]{2,1,0:T(8,128)(4,1)S(1)} %and.54) | copy-start | bytes 1769476
  552.9 151.1 %all-to-all-start.2 = ((bf16[4,128,2048]{2,1,0:T(8,128)(2,1)}), bf16[4,128,2048]{2,1,0:T(8,128)(2,1)}, u32[]{:S(2)}, u32[]{:S(2)}) async-start(bf16[4,128,2048]{2,1,0:T(8,128)(2,1)} %convert_element_type.253), calls=%async_computation.2 | async-start | bytes 4194304 | tf_op jit(solution)/shard_map/all_to_all | solution.py:142
  567.8 370.8 %reduce-scatter.12.cloned.1.call-start = ((), (), s32[]{:S(2)}) async-start(), calls=%async_computation.19 | async-start | bytes 17301504 | tf_op jit(solution)/shard_map/reduce_scatter | solution.py:232
  686.3 10.9 copy-start.2
  686.3 11.0 copy-start.27
  728.4 9.1 copy-start.48
  757.3 368.2 %reduce-scatter.10.cloned.1.call-start = ((), (), s32[]{:S(2)}) async-start(), calls=%async_computation.17 | async-start | bytes 17301504 | tf_op jit(solution)/shard_map/reduce_scatter | solution.py:233
  773.4 165.2 %copy-start.6 = (f32[128,2048]{1,0:T(8,128)S(1)}, f32[128,2048]{1,0:T(8,128)}, u32[]{:S(2)}) copy-start(f32[128,2048]{1,0:T(8,128)} %copy-done.5) | copy-start | bytes 3145732
  773.4 352.1 %copy-start.26 = (bf16[1,128,2048]{2,1,0:T(8,128)(2,1)S(1)}, bf16[1,128,2048]{2,1,0:T(8,128)(2,1)}, u32[]{:S(2)}) copy-start(bf16[1,128,2048]{2,1,0:T(8,128)(2,1)} %param.24) | copy-start | bytes 1572868
  773.4 610.7 %reduce-scatter.22.cloned.1.call-start = ((), (), s32[]{:S(2)}) async-start(), calls=%async_computation.25 | async-start | bytes 1081344
  1127.8 9.3 copy-start.17
  1127.9 9.3 copy-start.19
  1127.9 9.3 copy-start.21
  1127.9 9.3 copy-start.23
  1147.6 8.4 slice-start.4
  1156.0 5.6 copy-start.12
  1161.6 320.2 %reduce-scatter.20.cloned.1.call-start = ((), (), s32[]{:S(2)}) async-start(), calls=%async_computation.23 | async-start | bytes 8650752 | tf_op jit(solution)/shard_map/reduce_scatter | solution.py:299
  1167.2 461.6 %reduce-scatter.18.cloned.1.call-start = ((), (), s32[]{:S(2)}) async-start(), calls=%async_computation.22 | async-start | bytes 8650752 | tf_op jit(solution)/shard_map/reduce_scatter | solution.py:299
  1174.0 601.7 %reduce-scatter.16.cloned.1.call-start = ((), (), s32[]{:S(2)}) async-start(), calls=%async_computation.21 | async-start | bytes 8650752 | tf_op jit(solution)/shard_map/reduce_scatter | solution.py:299
  1179.8 743.0 %reduce-scatter.14.cloned.1.call-start = ((), (), s32[]{:S(2)}) async-start(), calls=%async_computation.20 | async-start | bytes 8650752 | tf_op jit(solution)/shard_map/reduce_scatter | solution.py:299
  1195.2 54.4 %all-to-all-start.5 = ((bf16[4,128,2048]{2,1,0:T(8,128)(2,1)}), bf16[4,128,2048]{2,1,0:T(8,128)(2,1)}, u32[]{:S(2)}, u32[]{:S(2)}) async-start(bf16[4,128,2048]{2,1,0:T(8,128)(2,1)} %bitcast.255), calls=%async_computation.11 | async-start | bytes 4194304 | tf_op jit(solution)/shard_map/all_to_all | solution.py:142
  1249.6 55.4 %all-to-all-start.3 = ((bf16[8,256,512]{2,1,0:T(8,128)(2,1)}), bf16[8,256,512]{2,1,0:T(8,128)(2,1)}, u32[]{:S(2)}, u32[]{:S(2)}) async-start(bf16[8,256,512]{2,1,0:T(8,128)(2,1)} %bitcast.254), calls=%async_computation.9 | async-start | bytes 4194304 | tf_op jit(solution)/shard_map/all_to_all | solution.py:133
  1305.0 59.2 %all-to-all-start.4 = ((bf16[8,256,512]{2,1,0:T(8,128)(2,1)}), bf16[8,256,512]{2,1,0:T(8,128)(2,1)}, u32[]{:S(2)}, u32[]{:S(2)}) async-start(bf16[8,256,512]{2,1,0:T(8,128)(2,1)} %bitcast.253), calls=%async_computation.10 | async-start | bytes 4194304 | tf_op jit(solution)/shard_map/all_to_all | solution.py:133
  1376.4 6.5 copy-start.13
  (26 other events, 62.1 us)
Sparse Core Ops, SparseCore 0:
  11.5 80.2 all-gather.11
  95.2 76.1 all-gather.9
  174.8 76.1 all-gather.7
  254.3 76.1 all-gather.13
  333.2 189.6 all-gather.15
  526.2 148.0 all-gather.17
  757.4 181.1 reduce-scatter.11
  940.9 184.5 reduce-scatter.9
  1161.7 140.8 reduce-scatter.21
  1304.9 176.8 reduce-scatter.19
  1484.2 144.5 reduce-scatter.17
  1631.1 144.5 reduce-scatter.15
  1778.1 144.6 reduce-scatter.13

commit v2 on v1

--- a/solution.py
+++ b/solution.py
@@ -1,8 +1,11 @@
+import functools
 import math
 
 import jax
 import jax.numpy as jnp
 from jax import lax
+from jax.experimental import pallas as pl
+from jax.experimental.pallas import tpu as pltpu
 from jax.sharding import PartitionSpec as P
 
 HEADS = 16
@@ -39,6 +42,409 @@
 
 
 AXES = ("dp", "expert")
+MESH = pl.DeviceIdType.MESH
+
+
+def torus(groups, group_size):
+    return 4, groups // 4, group_size // 2
+
+
+def place(sizes):
+    _, rows, columns = sizes
+    dp, ep = lax.axis_index("dp"), lax.axis_index("expert")
+    return dp // rows, lax.rem(dp, rows), ep // 2, lax.rem(ep, 2)
+
+
+def shift(index, step, size):
+    return lax.rem(index + step, size)
+
+
+def greet(sizes, spot):
+    na, nb, nc = sizes
+    a, b, c, k = spot
+    barrier = pltpu.get_barrier_semaphore()
+    peers = [(shift(a, s, na), b, c, k) for s in range(1, na)]
+    peers += [(a, shift(b, s, nb), c, k) for s in range(1, nb)]
+    peers += [(a, b, shift(c, s, nc), k) for s in range(1, nc)]
+    peers += [(a, b, c, 1 - k)]
+    for peer in peers:
+        pl.semaphore_signal(barrier, inc=1, device_id=address(sizes, peer), device_id_type=MESH)
+    pl.semaphore_wait(barrier, len(peers))
+
+
+def address(sizes, spot):
+    a, b, c, k = spot
+    return (a * sizes[1] + b, c * 2 + k)
+
+
+def gather_kernel(sizes, arrays, jobs, *refs):
+    na, nb, nc = sizes
+    count = len(jobs)
+    own_sem, send_sem, recv_sem, pair_send, pair_recv = refs[2 * arrays :]
+
+    def held(chunk):
+        array, start, rows = jobs[chunk]
+        return refs[array].at[pl.ds(start, rows)]
+
+    def landed(chunk, block):
+        array, start, rows = jobs[chunk]
+        return refs[arrays + array].at[index(*block), pl.ds(start, rows)]
+
+    spot = place(sizes)
+    a, b, c, k = spot
+
+    def index(a, b, c, k):
+        return (a * nb + b) * (2 * nc) + c * 2 + k
+
+    greet(sizes, spot)
+    sent = []
+
+    def half(ref, part):
+        if part is None:
+            return ref
+        rows = ref.shape[0] // 2
+        return ref.at[pl.ds(part * rows, rows)]
+
+    def slot(da, db, dc, part):
+        base = (da * nb + db) * nc + dc
+        return base if part is None or part == 0 else na * nb * nc + base
+
+    def push(chunk, source, peer, block, da, db, dc, part):
+        dst = landed(chunk, block)
+        n = len(sent)
+        copy = pltpu.make_async_remote_copy(
+            src_ref=half(source, part), dst_ref=half(dst, part),
+            send_sem=send_sem.at[n], recv_sem=recv_sem.at[chunk, slot(da, db, dc, part)],
+            device_id=address(sizes, peer), device_id_type=MESH)
+        copy.start()
+        sent.append(copy)
+
+    pairs = []
+
+    def pair(chunk, source, block, da, db, dc, part):
+        dst = landed(chunk, block)
+        copy = pltpu.make_async_remote_copy(
+            src_ref=half(source, part), dst_ref=half(dst, part),
+            send_sem=pair_send.at[len(pairs)], recv_sem=pair_recv.at[chunk, slot(da, db, dc, part)],
+            device_id=address(sizes, (a, b, c, 1 - k)), device_id_type=MESH)
+        copy.start()
+        pairs.append(copy)
+
+    def arrived(chunk, da, db, dc, part):
+        block = (shift(a, na - da, na), shift(b, nb - db, nb), shift(c, nc - dc, nc), k)
+        ref = landed(chunk, block)
+        view = half(ref, part)
+        pltpu.make_async_copy(view, view, recv_sem.at[chunk, slot(da, db, dc, part)]).wait()
+        return ref, block
+
+    def line(chunk, source, block, da):
+        for s in range(1, nb):
+            push(chunk, source, (a, shift(b, s, nb), c, k), block, da, s, 0, None)
+        for s in range(1, nc):
+            push(chunk, source, (a, b, shift(c, s, nc), k), block, da, 0, s, None)
+        pair(chunk, source, block, da, 0, 0, None)
+
+    def first(chunk):
+        block = (a, b, c, k)
+        for s in range(1, na):
+            push(chunk, held(chunk), (shift(a, s, na), b, c, k), block, s, 0, 0, None)
+        line(chunk, held(chunk), block, 0)
+
+    def second(chunk):
+        for da in range(1, na):
+            ref, block = arrived(chunk, da, 0, 0, None)
+            line(chunk, ref, block, da)
+
+    def third(chunk):
+        for da in range(na):
+            for db in range(1, nb):
+                ref, block = arrived(chunk, da, db, 0, None)
+                for s in range(1, nc):
+                    push(chunk, ref, (a, b, shift(c, s, nc), k), block, da, db, s, 0)
+                pair(chunk, ref, block, da, db, 0, None)
+            for dc in range(1, nc):
+                ref, block = arrived(chunk, da, 0, dc, None)
+                for s in range(1, nb):
+                    push(chunk, ref, (a, shift(b, s, nb), c, k), block, da, s, dc, 1)
+                pair(chunk, ref, block, da, 0, dc, None)
+
+    def fourth(chunk):
+        for da in range(na):
+            for db in range(1, nb):
+                for dc in range(1, nc):
+                    for part in (0, 1):
+                        ref, block = arrived(chunk, da, db, dc, part)
+                        pair(chunk, ref, block, da, db, dc, part)
+
+    own = []
+    for chunk in range(count):
+        first(chunk)
+        copy = pltpu.make_async_copy(
+            held(chunk), landed(chunk, (a, b, c, k)), own_sem.at[chunk])
+        copy.start()
+        own.append(copy)
+    for step in range(count + 2):
+        if step < count:
+            second(step)
+        if 0 <= step - 1 < count:
+            third(step - 1)
+        if 0 <= step - 2 < count:
+            fourth(step - 2)
+    for chunk in range(count):
+        own[chunk].wait()
+        for da in range(na):
+            for db in range(nb):
+                for dc in range(nc):
+                    for part in (0, 1) if db and dc else (None,):
+                        block = (shift(a, na - da, na), shift(b, nb - db, nb), shift(c, nc - dc, nc), 1 - k)
+                        view = half(landed(chunk, block), part)
+                        pltpu.make_async_copy(
+                            view, view, pair_recv.at[chunk, slot(da, db, dc, part)]).wait()
+    for copy in sent:
+        copy.wait_send()
+    for copy in pairs:
+        copy.wait_send()
+
+
+def gather_all(blocks, pieces, collective_id):
+    groups, group_size = lax.axis_size("dp"), lax.axis_size("expert")
+    sizes = torus(groups, group_size)
+    na, nb, nc = sizes
+    arrays = len(blocks)
+    total = na * nb * nc
+    jobs = []
+    for array, block in enumerate(blocks):
+        cuts = max(1, min(pieces, block.shape[0] // 32, 128 // total))
+        rows = block.shape[0] // cuts
+        jobs += [(array, rows * cut, rows) for cut in range(cuts)]
+    count = len(jobs)
+    diag = na * (nb - 1) * (nc - 1)
+    sends = count * (na - 1 + na * (nb - 1) + na * (nc - 1) + 2 * diag)
+    pair_sends = count * (total + diag)
+    dma = pltpu.SemaphoreType.DMA
+    return pl.pallas_call(
+        functools.partial(gather_kernel, sizes, arrays, tuple(jobs)),
+        out_shape=[jax.ShapeDtypeStruct((groups * group_size,) + x.shape, x.dtype) for x in blocks],
+        in_specs=[pl.BlockSpec(memory_space=pltpu.VMEM)] * arrays,
+        out_specs=[pl.BlockSpec(memory_space=pl.ANY)] * arrays,
+        scratch_shapes=[dma((count,)), dma((sends,)), dma((count, 2 * total)), dma((pair_sends,)),
+                        dma((count, 2 * total))],
+        compiler_params=pltpu.CompilerParams(collective_id=collective_id, has_side_effects=True),
+    )(*blocks)
+
+
+def loop(size, body):
+    lax.fori_loop(0, size, lambda i, _: (body(i), None)[1], None)
+
+
+def reduce_kernel(sizes, jobs, take, *refs):
+    na, nb, nc = sizes
+    plane = nb * nc
+    total = na * plane
+    count = len(jobs)
+    (lhs, rhs, out, pair_out, held, diag_x, diag_y, from_x, from_y, from_z,
+     pair_s, pair_r, dx_s, dx_r, dy_s, dy_r, x_s, x_r, y_s, y_r, z_s, z_r) = refs
+    spot = place(sizes)
+    a, b, c, k = spot
+    rows = held.shape[2]
+    part = rows // 2
+    low, wide = held.dtype, jnp.float32
+    greet(sizes, spot)
+
+    def number(aa, bb, cc):
+        return (aa * nb + bb) * nc + cc
+
+    def mine(chunk, n, core):
+        bb, cc = lax.rem(n // nc, nb), lax.rem(n, nc)
+        block = (n // plane * nb + bb) * (2 * nc) + cc * 2 + core
+        page, start = take(jobs[chunk], block)
+        left_page, right_page = page if isinstance(page, tuple) else (page, page)
+        left = lhs[left_page, pl.ds(pl.multiple_of(start, part), rows)]
+        return jnp.dot(left, rhs[right_page], preferred_element_type=wide)
+
+    def send(src, dst, s_sem, r_sem, peer):
+        pltpu.make_async_remote_copy(
+            src_ref=src, dst_ref=dst, send_sem=s_sem, recv_sem=r_sem,
+            device_id=address(sizes, peer), device_id_type=MESH).start()
+
+    def wait(view, sem):
+        pltpu.make_async_copy(view, view, sem).wait()
+
+    first, last = pl.ds(0, part), pl.ds(part, part)
+
+    def stage_pair(chunk):
+        slot = chunk % 2
+        def one(aa):
+            ref = pair_out.at[slot, pl.ds(aa * plane, plane)]
+            if chunk >= 2:
+                wait(ref, pair_s.at[slot, aa])
+            def fill(m):
+                n = aa * plane + m
+                pair_out[slot, n] = mine(chunk, n, 1 - k).astype(low)
+            loop(plane, fill)
+            send(ref, held.at[chunk, pl.ds(aa * plane, plane)], pair_s.at[slot, aa], pair_r.at[chunk, aa],
+                 (a, b, c, 1 - k))
+        loop(na, one)
+
+    def stage_diag(chunk):
+        def one(aa):
+            wait(held.at[chunk, pl.ds(aa * plane, plane)], pair_r.at[chunk, aa])
+            def add(m):
+                n = aa * plane + m
+                held[chunk, n] = (held[chunk, n].astype(wide) + mine(chunk, n, k)).astype(low)
+            loop(plane, add)
+            for db in range(1, nb):
+                bb = shift(b, db, nb)
+                for dc in range(1, nc):
+                    cc = shift(c, dc, nc)
+                    m = (db - 1) * (nc - 1) + dc - 1
+                    n = number(aa, bb, cc)
+                    send(held.at[chunk, n, last], diag_x.at[chunk, m, aa], dx_s.at[chunk, m, aa],
+                         dx_r.at[chunk, m, aa], (a, bb, c, k))
+                    send(held.at[chunk, n, first], diag_y.at[chunk, m, aa], dy_s.at[chunk, m, aa],
+                         dy_r.at[chunk, m, aa], (a, b, cc, k))
+            for db in range(1, nb):
+                bb = shift(b, db, nb)
+                send(held.at[chunk, number(aa, bb, c), last], from_x.at[chunk, db - 1, aa, last],
+                     x_s.at[chunk, db - 1, aa, 1], x_r.at[chunk, db - 1, aa, 1], (a, bb, c, k))
+            for dc in range(1, nc):
+                cc = shift(c, dc, nc)
+                send(held.at[chunk, number(aa, b, cc), first], from_y.at[chunk, dc - 1, aa, first],
+                     y_s.at[chunk, dc - 1, aa, 0], y_r.at[chunk, dc - 1, aa, 0], (a, b, cc, k))
+        loop(na, one)
+
+    def stage_turn(chunk):
+        def one(aa):
+            for db in range(1, nb):
+                bb = shift(b, db, nb)
+                n = number(aa, bb, c)
+                value = held[chunk, n, first].astype(wide)
+                for dc in range(1, nc):
+                    m = (db - 1) * (nc - 1) + dc - 1
+                    wait(diag_y.at[chunk, m, aa], dy_r.at[chunk, m, aa])
+                    value += diag_y[chunk, m, aa].astype(wide)
+                held[chunk, n, first] = value.astype(low)
+                send(held.at[chunk, n, first], from_x.at[chunk, db - 1, aa, first],
+                     x_s.at[chunk, db - 1, aa, 0], x_r.at[chunk, db - 1, aa, 0], (a, bb, c, k))
+            for dc in range(1, nc):
+                cc = shift(c, dc, nc)
+                n = number(aa, b, cc)
+                value = held[chunk, n, last].astype(wide)
+                for db in range(1, nb):
+                    m = (db - 1) * (nc - 1) + dc - 1
+                    wait(diag_x.at[chunk, m, aa], dx_r.at[chunk, m, aa])
+                    value += diag_x[chunk, m, aa].astype(wide)
+                held[chunk, n, last] = value.astype(low)
+                send(held.at[chunk, n, last], from_y.at[chunk, dc - 1, aa, last],
+                     y_s.at[chunk, dc - 1, aa, 1], y_r.at[chunk, dc - 1, aa, 1], (a, b, cc, k))
+        loop(na, one)
+
+    def stage_line(chunk):
+        def one(da):
+            aa = shift(a, da + 1, na)
+            n = number(aa, b, c)
+            value = held[chunk, n].astype(wide)
+            for db in range(nb - 1):
+                for side, where in ((1, last), (0, first)):
+                    wait(from_x.at[chunk, db, aa, where], x_r.at[chunk, db, aa, side])
+                value += from_x[chunk, db, aa].astype(wide)
+            for dc in range(nc - 1):
+                for side, where in ((0, first), (1, last)):
+                    wait(from_y.at[chunk, dc, aa, where], y_r.at[chunk, dc, aa, side])
+                value += from_y[chunk, dc, aa].astype(wide)
+            held[chunk, n] = value.astype(low)
+            @pl.when(da < na - 1)
+            def _():
+                send(held.at[chunk, n], from_z.at[chunk, da], z_s.at[chunk, da], z_r.at[chunk, da], (aa, b, c, k))
+        loop(na, one)
+
+    def stage_end(chunk):
+        value = held[chunk, number(a, b, c)].astype(wide)
+        for da in range(na - 1):
+            wait(from_z.at[chunk, da], z_r.at[chunk, da])
+            value += from_z[chunk, da].astype(wide)
+        out[chunk] = value.astype(out.dtype)
+
+    stages = (stage_pair, stage_diag, stage_turn, stage_line, stage_end)
+    lags = (0, 1, 2, 3, 4)
+    for step in range(count + lags[-1]):
+        for stage, lag in zip(stages, lags):
+            if 0 <= step - lag < count:
+                stage(step - lag)
+
+    for chunk in range(count):
+        def one(aa):
+            if chunk >= count - 2:
+                wait(pair_out.at[chunk % 2, pl.ds(aa * plane, plane)], pair_s.at[chunk % 2, aa])
+            for m in range((nb - 1) * (nc - 1)):
+                wait(diag_x.at[chunk, m, aa], dx_s.at[chunk, m, aa])
+                wait(diag_y.at[chunk, m, aa], dy_s.at[chunk, m, aa])
+            for db in range(nb - 1):
+                wait(from_x.at[chunk, db, aa, first], x_s.at[chunk, db, aa, 0])
+                wait(from_x.at[chunk, db, aa, last], x_s.at[chunk, db, aa, 1])
+            for dc in range(nc - 1):
+                wait(from_y.at[chunk, dc, aa, first], y_s.at[chunk, dc, aa, 0])
+                wait(from_y.at[chunk, dc, aa, last], y_s.at[chunk, dc, aa, 1])
+        loop(na, one)
+        def two(da):
+            wait(from_z.at[chunk, da], z_s.at[chunk, da])
+        loop(na - 1, two)
+
+
+def reduce_call(lhs, rhs, jobs, take, rows, collective_id):
+    groups, group_size = lax.axis_size("dp"), lax.axis_size("expert")
+    sizes = torus(groups, group_size)
+    na, nb, nc = sizes
+    total = na * nb * nc
+    width = rhs.shape[-1]
+    count = len(jobs)
+    low = jnp.bfloat16
+    diag = (nb - 1) * (nc - 1)
+    dma = pltpu.SemaphoreType.DMA
+    both = lambda *shape: [dma(shape), dma(shape)]
+    return pl.pallas_call(
+        functools.partial(reduce_kernel, sizes, jobs, take),
+        out_shape=jax.ShapeDtypeStruct((count, rows, width), jnp.float32),
+        in_specs=[pl.BlockSpec(memory_space=pltpu.VMEM)] * 2,
+        out_specs=pl.BlockSpec(memory_space=pltpu.VMEM),
+        scratch_shapes=[
+            pltpu.VMEM((2, total, rows, width), low),
+            pltpu.VMEM((count, total, rows, width), low),
+            pltpu.VMEM((count, diag, na, rows // 2, width), low),
+            pltpu.VMEM((count, diag, na, rows // 2, width), low),
+            pltpu.VMEM((count, nb - 1, na, rows, width), low),
+            pltpu.VMEM((count, nc - 1, na, rows, width), low),
+            pltpu.VMEM((count, na - 1, rows, width), low),
+            dma((2, na)), dma((count, na)),
+            *both(count, diag, na), *both(count, diag, na),
+            *both(count, nb - 1, na, 2), *both(count, nc - 1, na, 2),
+            *both(count, na - 1),
+        ],
+        compiler_params=pltpu.CompilerParams(collective_id=collective_id, has_side_effects=True,
+                                             vmem_limit_bytes=64_000_000),
+    )(lhs, rhs)
+
+
+def padded(array):
+    return math.prod(array.shape[:-1]) * (-(-array.shape[-1] // 128) * 128) * array.dtype.itemsize
+
+
+def reduce_all(lhs, rhs, jobs, take, rows, collective_id):
+    groups, group_size = lax.axis_size("dp"), lax.axis_size("expert")
+    na, nb, nc = torus(groups, group_size)
+    total = na * nb * nc
+    line = rows * rhs.shape[-1] * 2
+    diag = (nb - 1) * (nc - 1)
+    each = line * (total + diag * na + (nb - 1 + nc - 1) * na + na - 1) + 2 * line
+    spare = 58_000_000 - padded(lhs) - padded(rhs) - 2 * total * line
+    fit = max(1, spare // each)
+    calls = -(-len(jobs) // fit)
+    size = -(-len(jobs) // calls)
+    parts = [
+        reduce_call(lhs, rhs, tuple(jobs[at : at + size]), take, rows, collective_id + at)
+        for at in range(0, len(jobs), size)
+    ]
+    return parts[0] if len(parts) == 1 else jnp.concatenate(parts, axis=0)
 
 
 def expert_tables(routes, gates, expert, capacity):
@@ -147,12 +553,10 @@
     up_mat = to_owner(w_up)
     down_mat = swap_down(w_down.astype(low)).reshape(hidden_part, width)
 
-    attn_mats = (
-        lax.all_gather(w_query.astype(low), AXES, axis=0, tiled=True),
-        lax.all_gather(w_key.astype(low), AXES, axis=0, tiled=True),
-        lax.all_gather(w_value.astype(low), AXES, axis=0, tiled=True),
-        lax.all_gather(w_out.astype(low), AXES, axis=0, tiled=True),
-    )
+    attn_mats = gather_all(
+        [w_query.astype(low), w_key.astype(low), w_value.astype(low), w_out.astype(low)], 2, 1
+    )
+    attn_mats = [mat.reshape(width, width) for mat in attn_mats]
     query_mat, key_mat, value_mat, out_mat = attn_mats
     all_cotangent = lax.all_gather(cotangent, AXES, axis=0, tiled=True)
     scale_in = norm_scale(seq_inputs)
@@ -191,7 +595,7 @@
     scale_mid = norm_scale(residual)
     normed_mid = residual * scale_mid
     hidden_mid = (normed_mid * ffn_gain).astype(jnp.bfloat16)
-    all_hidden = lax.all_gather(hidden_mid[None], AXES, axis=0, tiled=True)
+    (all_hidden,) = gather_all([hidden_mid], 4, 2)
     bundled = all_hidden.reshape(bundles, joined * length_rows, width)
     rows = jnp.einsum("bct,btd->bcd", select, bundled, preferred_element_type=wide).astype(low)
     rows = rows.reshape(total_rows, width)
@@ -211,8 +615,6 @@
             bundles, joined * capacity, width
         )
     ).astype(low)
-    out_part = jnp.einsum("bct,bcd->btd", select, expert_out, preferred_element_type=wide)
-    out_part = out_part.astype(low).reshape(seqs, length_rows, width)
     grad_hidden = jnp.einsum("md,fd->mf", out_grads, down_mat, preferred_element_type=wide)
     grad_gate_pre = (
         grad_hidden * up_pre * sigmoid_gate * (1.0 + gate_pre * (1.0 - sigmoid_gate))
@@ -222,15 +624,24 @@
         jnp.einsum("mf,df->md", grad_gate_pre, gate_mat, preferred_element_type=wide)
         + jnp.einsum("mf,df->md", grad_up_pre, up_mat, preferred_element_type=wide)
     ).astype(low)
-    mid_part = jnp.einsum(
-        "bct,bcd->btd",
-        select,
+    placed = select.transpose(0, 2, 1)
+    cuts = max(1, min(4, 128 // (seqs // 2)))
+    cut_rows = length_rows // cuts if seqs <= 32 else 16
+    token_jobs = [(0, start) for start in range(0, length_rows, cut_rows)]
+
+    def token_take(job, block):
+        return block // joined, lax.rem(block, joined) * length_rows + job[1]
+
+    grad_mid = reduce_all(
+        placed,
         grad_slots.reshape(bundles, joined * capacity, width),
-        preferred_element_type=wide,
-    )
-    mid_part = mid_part.astype(low).reshape(seqs, length_rows, width)
-    grad_mid = lax.psum_scatter(mid_part, AXES, scatter_dimension=0, tiled=True)[0].astype(wide)
-    mixture = lax.psum_scatter(out_part, AXES, scatter_dimension=0, tiled=True)[0].astype(wide)
+        token_jobs,
+        token_take,
+        cut_rows,
+        10,
+    ).reshape(length_rows, width)
+    mixture = reduce_all(placed, expert_out, token_jobs, token_take, cut_rows, 30)
+    mixture = mixture.reshape(length_rows, width)
     layer_rows = (residual + mixture).astype(low)
     grad_down = jnp.einsum("mf,md->fd", hidden_act, out_grads, preferred_element_type=wide)
     grad_gate = jnp.einsum("md,mf->df", rows, grad_gate_pre, preferred_element_type=wide)
@@ -243,7 +654,6 @@
     ffn_gain_part = jnp.sum(grad_mid * normed_mid, axis=0)
     grad_resid = seq_grads + norm_back(normed_mid, scale_mid, grad_mid * ffn_gain)
     resid_low = grad_resid.astype(jnp.bfloat16)
-    grad_out_mat = jnp.einsum("td,te->de", attended, resid_low, preferred_element_type=jnp.float32)
     grad_attended = jnp.einsum(
         "te,de->td", resid_low, out_mat, preferred_element_type=jnp.float32
     ).astype(jnp.bfloat16)
@@ -274,15 +684,6 @@
         jnp.bfloat16
     )
     grad_key_raw = norm_back(key_normed, key_scale, key_turned * key_gain).astype(jnp.bfloat16)
-    grad_query_mat = jnp.einsum(
-        "td,te->de", hidden_in, grad_query_raw, preferred_element_type=jnp.float32
-    )
-    grad_key_mat = jnp.einsum(
-        "td,te->de", hidden_in, grad_key_raw, preferred_element_type=jnp.float32
-    )
-    grad_value_mat = jnp.einsum(
-        "td,te->de", hidden_in, grad_values, preferred_element_type=jnp.float32
-    )
     grad_hidden_in = jnp.einsum(
         "te,de->td", grad_query_raw, query_mat, preferred_element_type=jnp.float32
     )
@@ -295,21 +696,32 @@
     attn_gain_part = jnp.sum(grad_hidden_in * normed_in, axis=0)
     grad_seq = grad_resid + norm_back(normed_in, scale_in, grad_hidden_in * attn_gain)
 
-    def to_rows(grad):
-        return lax.psum_scatter(grad.astype(low), AXES, scatter_dimension=0, tiled=True).astype(wide)
-
+    lhs = jnp.stack([hidden_in.T, attended.T])
+    rhs = jnp.stack([grad_query_raw, grad_key_raw, grad_values, resid_low])
+    held_rows = w_query.shape[0]
+    weight_cuts = max(1, min(2, held_rows // 32))
+    weight_rows = held_rows // weight_cuts
+    weight_jobs = [
+        (mat, cut * weight_rows) for mat in (3, 2, 1, 0) for cut in range(weight_cuts)
+    ]
+
+    def weight_take(job, block):
+        return (1 if job[0] == 3 else 0, job[0]), block * held_rows + job[1]
+
+    weight_grads = reduce_all(lhs, rhs, weight_jobs, weight_take, weight_rows, 50)
+    weight_grads = weight_grads.reshape(4, held_rows, width)
     gain_parts = jnp.stack([attn_gain_part, query_gain_part, key_gain_part, ffn_gain_part])
     gains = lax.psum_scatter(gain_parts, AXES, scatter_dimension=1, tiled=True)
     return (
         layer_rows[None],
         grad_seq.astype(low)[None],
         gains[0],
-        to_rows(grad_query_mat),
-        to_rows(grad_key_mat),
-        to_rows(grad_value_mat),
+        weight_grads[3],
+        weight_grads[2],
+        weight_grads[1],
         gains[1],
         gains[2],
-        to_rows(grad_out_mat),
+        weight_grads[0],
         gains[3],
         *expert_grads,
     )

time: 1940 us -> 1160 us (0.60)
  waiting for transfers between devices: 1450 us -> 40.5 us
  Pallas kernels: 0 us -> 693 us
  matrix products: 212 us -> 163 us
  blocking collectives: 108 us -> 78.9 us
    reduce_scatter x6 -> x0, waiting for transfers between devices: 880 us -> none  [the longest x4 530 us: to_rows(): lax.psum_scatter(grad.astype(low), AXES, scatter_dimension=0, tiled=True)]
    pallas_call x0 -> x5, Pallas kernels: none -> 693 us  [the longest x3 380 us: reduce_call(): pl.pallas_call(functools.partial(reduce_kernel, sizes, jobs, take), out_s...]
    all_gather x5 -> x0, waiting for transfers between devices: 379 us -> none  [the longest x1 90 us: per_device(): all_hidden = lax.all_gather(hidden_mid[None], AXES, axis=0, tiled=True)]
    all_to_all x2, waiting for transfers between devices: 71.7 us -> 0.01 us  [to_owner(): mat = lax.all_to_all(mat, 'dp', split_axis=0, concat_axis=0, tiled=True)]
    all_to_all x2, waiting for transfers between devices: 73.5 us -> 26.4 us  [to_master(): grad = lax.all_to_all(grad, 'dp', split_axis=0, concat_axis=0, tiled=True)]
    dot_general x6 -> x1, matrix products: 46.3 us -> 9.11 us  [per_device(): jnp.dot(hidden_act, down_mat, preferred_element_type=wide)]
    all_gather x1, blocking collectives: 108 us -> 78.9 us  [per_device(): tables = lax.all_gather(payload, AXES, axis=0, tiled=False)]
    all_to_all x2, waiting for transfers between devices: 40.6 us -> 13.4 us  [swap_down(): lax.all_to_all(mat, 'dp', split_axis=0, concat_axis=0, axis_index_groups=...]
  transfers between devices with their start and end apart: 19 -> 8, of which waited for: 15 -> 2; matrix products, arithmetic and copies ran while one was open for 12% -> 21% of each run, Pallas kernels for 0% -> 60%
where the time goes in v2:
time: 1160 us; the launch traced here: 1150 us
  Pallas kernels  693 us (60%)
  matrix products  163 us (14%)
  local copies, waits for them, and re-layouts  85 us (7%)
  blocking collectives  78.9 us (7%)
  starting transfers between devices  41.4 us (4%)
  waiting for transfers between devices  40.5 us (3%)
  other arithmetic  36.8 us (3%)
  between operations  15.5 us (1%)
    pallas_call x3, Pallas kernels, reduce_call(): pl.pallas_call(functools.partial(reduce_kernel, sizes, jobs, take), out_s...  380 us
    pallas_call x2, Pallas kernels, gather_all(): pl.pallas_call(functools.partial(gather_kernel, sizes, arrays, tuple(jobs...  313 us
    all_gather x1, blocking collectives, per_device(): tables = lax.all_gather(payload, AXES, axis=0, tiled=False)  78.9 us
    convert_element_type x6, local copies, waits for them, and re-layouts, to_master(): grad.transpose(0, 2, 3, 1, 4).reshape(local_experts, rows_held, hidden)  35.5 us
    all_to_all x2, waiting for transfers between devices, to_master(): grad = lax.all_to_all(grad, 'dp', split_axis=0, concat_axis=0, tiled=True)  26.4 us
  transfers between devices with their start and end apart: 8, of which 2 were waited for; matrix products, arithmetic and copies ran while one was open for 21% of the time, Pallas kernels for 60%

profile of v2, /device:TPU:0, one launch (start us, length us, event | category | flops | bytes accessed | tf_op | source)
XLA Modules:
  0.0 1154.2 jit_solution(10243160238886042745)
XLA Ops:
  7.9 3.3 copy.202
  12.8 7.4 all-to-all-start
  23.4 78.9 %all_gather.13 = f32[32,24,128]{2,1,0:T(8,128)S(1)} all-gather(f32[1,24,128]{2,1,0:T(8,128)S(1)} %scatter.14), channel_id=1, replica_groups=mesh['dp'=8,'expert'=4] {'dp','expert'}, dimensions={0}, use_global_device_ids=true | all-gather | bytes 405504 | tf_op jit(solution)/shard_map/all_gather | solution.py:509
  104.0 196.4 %shard_map.264 = (bf16[32,64,2048]{2,1,0:T(8,128)(2,1)}, bf16[32,64,2048]{2,1,0:T(8,128)(2,1)}, bf16[32,64,2048]{2,1,0:T(8,128)(2,1)}, bf16[32,64,2048]{2,1,0:T(8,128)(2,1)}) custom-call(bf16[64,2048]{1,0:T(8,128)(2,1)} %convert_element_type.206.refs_0_, bf16[64,2048]{1,0:T(8,128)(2,1)} %convert_element_type.207.refs_1_, ...), custom_call_target="tpu_custom_call" | custom-call | tf_op jit(solution)/shard_map/pallas_call | solution.py:225
  300.6 4.8 multiply_reduce_fusion.6
  308.7 4.8 copy.205
  313.5 3.1 copy.206
  317.0 4.8 multiply_reduce_fusion.5
  332.6 13.5 %all-to-all-start.1 = ((bf16[8,256,512]{1,2,0:T(8,128)(2,1)}), bf16[8,256,512]{1,2,0:T(8,128)(2,1)}, u32[]{:S(2)}, u32[]{:S(2)}) async-start(bf16[8,256,512]{1,2,0:T(8,128)(2,1)} %bitcast.274), calls=%async_computation.1 | async-start | bytes 4194304 | tf_op jit(solution)/shard_map/all_to_all | solution.py:534
  346.9 2.9 copy.201
  349.8 3.8 convert_element_type.228
  358.8 4.8 multiply_reduce_fusion.4
  364.6 117.0 %shard_map.265 = bf16[32,128,2048]{2,1,0:T(8,128)(2,1)} custom-call(bf16[128,2048]{1,0:T(8,128)(2,1)} %multiply_convert_fusion.8.refs_0_), custom_call_target="tpu_custom_call" | custom-call | tf_op jit(solution)/shard_map/pallas_call | solution.py:225
  483.3 12.0 %convolution_convert_fusion = bf16[16,144,2048]{2,1,0:T(8,128)(2,1)} fusion(pred[16,144,256]{2,1,0:T(8,128)(4,1)S(1)} %broadcast_and_fusion, bf16[16,256,2048]{2,1,0:T(8,128)(2,1)} %bitcast.242), kind=kOutput, calls=%fused_computation.5 | convolution fusion | flops 2420637696 | bytes 26804224 | tf_op jit(solution)/shard_map/bct,btd->bcd/dot_general | solution.py:600
  495.4 4.0 copy.204
  499.3 6.0 all-to-all-start.2
  505.4 4.0 copy.207
  509.4 10.9 fusion.66
  520.3 6.7 fusion.65
  527.0 14.0 %multiply_convert_fusion = bf16[16,144,2048]{2,1,0:T(8,128)(2,1)} fusion(f32[16,144]{1,0:T(8,128)S(1)} %mul.584, pred[16,144,256]{2,1,0:T(8,128)(4,1)S(1)} %broadcast_and_fusion, bf16[16,256,2048]{2,1,0:T(8,128)(2,1)} %bitcast.253), kind=kOutput, calls=%fused_computation.3 | convolution fusion | flops 2425356288 | bytes 26813440 | tf_op jit(solution)/shard_map/bct,btd->bcd/dot_general | solution.py:605
  541.0 13.4 %all-to-all-done.2 = bf16[4,128,2048]{2,1,0:T(8,128)(2,1)} async-done(((bf16[4,128,2048]{2,1,0:T(8,128)(2,1)}), bf16[4,128,2048]{2,1,0:T(8,128)(2,1)}, u32[]{:S(2)}, u32[]{:S(2)}) %all-to-all-start.2) | async-done | bytes 2097184 | tf_op jit(solution)/shard_map/all_to_all | solution.py:548
  554.4 13.8 %multiply_convert_fusion.2 = (bf16[2304,512]{1,0:T(8,128)(2,1)}, bf16[2304,512]{1,0:T(8,128)(2,1)}, bf16[2304,512]{1,0:T(8,128)(2,1)S(1)}) fusion(f32[2304,512]{1,0:T(8,128)} %fusion.65, f32[2304,512]{1,0:T(8,128)} %fusion.66, bf16[2304,2048]{1,0:T(8,128)(2,1)} %bitcast.254, bf16[512,2048]{1,0:T(8,128)(2,1)} %bitcast.31), kind=kOutput, calls=%fused_computation.6 | convolution fusion | flops 4850712576 | bytes 28049408 | tf_op jit(solution)/shard_map/md,fd->mf/dot_general | solution.py:618
  568.2 6.3 convolution_convert_fusion.1
  574.6 4.7 all-to-all-start.5
  579.3 11.2 fusion.67
  590.4 9.1 multiply_convert_fusion.1.refs_1_
  599.5 101.3 %shard_map.266 = f32[4,32,2048]{2,1,0:T(8,128)} custom-call(bf16[16,256,144]{2,1,0:T(8,128)(2,1)} %convert_bitcast_fusion.refs_0_, bf16[16,144,2048]{2,1,0:T(8,128)(2,1)} %multiply_convert_fusion.1.refs_1_), custom_call_target="tpu_custom_call" | custom-call | tf_op jit(solution)/shard_map/pallas_call | solution.py:405
  700.9 12.6 %add_convert_fusion = bf16[2304,2048]{1,0:T(8,128)(2,1)} fusion(f32[2304,2048]{1,0:T(8,128)} %fusion.67, bf16[2304,512]{1,0:T(8,128)(2,1)} %get-tuple-element.71, bf16[2048,512]{1,0:T(8,128)(2,1)} %bitcast.287), kind=kOutput, calls=%fused_computation.2 | convolution fusion | flops 4841275392 | bytes 32768000 | tf_op jit(solution)/shard_map/mf,df->md/dot_general | solution.py:625
  713.4 101.2 %shard_map.267 = f32[4,32,2048]{2,1,0:T(8,128)} custom-call(bf16[16,256,144]{2,1,0:T(8,128)(2,1)} %convert_bitcast_fusion.refs_0_, bf16[16,144,2048]{2,1,0:T(8,128)(2,1)} %bitcast.268), custom_call_target="tpu_custom_call" | custom-call | tf_op jit(solution)/shard_map/pallas_call | solution.py:405
  819.8 6.4 convolution_convert_fusion.4
  833.9 6.2 convolution_convert_fusion.3
  840.1 6.1 all-to-all-start.3
  848.5 2.9 multiply_convert_fusion.5
  852.0 7.4 fusion.68
  859.4 6.3 convolution_convert_fusion.2
  865.7 26.4 %all-to-all-done.3 = bf16[8,256,512]{2,1,0:T(8,128)(2,1)} async-done(((bf16[8,256,512]{2,1,0:T(8,128)(2,1)}), bf16[8,256,512]{2,1,0:T(8,128)(2,1)}, u32[]{:S(2)}, u32[]{:S(2)}) %all-to-all-start.3) | async-done | bytes 2097184 | tf_op jit(solution)/shard_map/all_to_all | solution.py:539
  892.2 3.6 all-to-all-start.4
  895.8 3.6 convolution_convert_fusion.6
  901.5 6.7 convolution_add_fusion.1
  908.3 6.6 fusion.19
  923.9 177.1 %shard_map.268 = f32[8,32,2048]{2,1,0:T(8,128)} custom-call(bf16[2,2048,128]{2,1,0:T(8,128)(2,1)} %copy.221.refs_0_, bf16[4,128,2048]{2,1,0:T(8,128)(2,1)} %pad_maximum_fusion.refs_1_), custom_call_target="tpu_custom_call" | custom-call | tf_op jit(solution)/shard_map/pallas_call | solution.py:405
  1107.2 4.1 convert_element_type.259
  1111.4 4.7 reshape.512
  1116.1 7.4 copy.281
  1123.5 6.4 reshape.510
  1129.9 3.2 reshape.513
  1133.1 7.4 copy.280
  1140.5 6.4 reshape.511
  (230 shorter events, 62.9 us)
Async XLA Ops:
  7.2 519.9 %all-gather.2.cloned.1.call-start = ((), (), s32[]{:S(2)}) async-start(), calls=%async_computation.7 | async-start | bytes 17301504 | tf_op jit(solution)/shard_map/all_gather | solution.py:561
  11.3 8.9 copy-start.31
  11.3 9.7 copy-start.32
  12.7 8.9 copy-start.33
  12.7 9.6 copy-start.34
  12.8 10.4 copy-start.47
  12.8 10.4 copy-start.49
  12.8 10.4 copy-start.48
  12.8 287.6 %copy-start = (bf16[1,128,2048]{2,1,0:T(8,128)(2,1)S(1)}, bf16[1,128,2048]{2,1,0:T(8,128)(2,1)}, u32[]{:S(2)}) copy-start(bf16[1,128,2048]{2,1,0:T(8,128)(2,1)} %param.23) | copy-start | bytes 1572868
  12.8 287.8 %copy-start.28 = (f32[2048]{0:T(1024)S(1)}, f32[2048]{0:T(1024)}, u32[]{:S(2)}) copy-start(f32[2048]{0:T(1024)} %param.29) | copy-start | bytes 24580
  12.8 319.8 %all-to-all-start = ((bf16[8,256,512]{1,2,0:T(8,128)(2,1)}), bf16[8,256,512]{1,2,0:T(8,128)(2,1)}, u32[]{:S(2)}, u32[]{:S(2)}) async-start(bf16[8,256,512]{1,2,0:T(8,128)(2,1)} %bitcast.273), calls=%async_computation | async-start | bytes 4194304 | tf_op jit(solution)/shard_map/all_to_all | solution.py:534
  300.6 29.9 %copy-start.40 = (f32[128]{0:T(128)}, f32[128]{0:T(128)S(1)}, u32[]{:S(2)}) copy-start(f32[128]{0:T(128)S(1)} %add_rsqrt_fusion.3) | copy-start | bytes 1540
  305.4 11.2 copy-start.3
  305.4 11.2 copy-start.43
  308.7 8.0 copy-start.38
  317.0 7.1 copy-start.50
  330.4 23.2 %copy-start.21 = (bf16[128,16,64]{2,0,1:T(8,128)(2,1)}, bf16[128,16,64]{2,0,1:T(8,128)(2,1)S(1)}, u32[]{:S(2)}) copy-start(bf16[128,16,64]{2,0,1:T(8,128)(2,1)S(1)} %get-tuple-element.96) | copy-start | bytes 786436
  330.4 25.1 %copy-start.15 = (bf16[128,16,64]{2,0,1:T(8,128)(2,1)}, bf16[128,16,64]{2,0,1:T(8,128)(2,1)S(1)}, u32[]{:S(2)}) copy-start(bf16[128,16,64]{2,0,1:T(8,128)(2,1)S(1)} %get-tuple-element.74) | copy-start | bytes 786436
  330.4 25.1 %copy-start.17 = (bf16[128,16,64]{2,0,1:T(8,128)(2,1)}, bf16[128,16,64]{2,0,1:T(8,128)(2,1)S(1)}, u32[]{:S(2)}) copy-start(bf16[128,16,64]{2,0,1:T(8,128)(2,1)S(1)} %get-tuple-element.75) | copy-start | bytes 786436
  330.5 25.1 %copy-start.19 = (bf16[128,16,64]{2,0,1:T(8,128)(2,1)}, bf16[128,16,64]{2,0,1:T(8,128)(2,1)S(1)}, u32[]{:S(2)}) copy-start(bf16[128,16,64]{2,0,1:T(8,128)(2,1)S(1)} %get-tuple-element.95) | copy-start | bytes 786436
  332.6 166.7 %all-to-all-start.1 = ((bf16[8,256,512]{1,2,0:T(8,128)(2,1)}), bf16[8,256,512]{1,2,0:T(8,128)(2,1)}, u32[]{:S(2)}, u32[]{:S(2)}) async-start(bf16[8,256,512]{1,2,0:T(8,128)(2,1)} %bitcast.274), calls=%async_computation.1 | async-start | bytes 4194304 | tf_op jit(solution)/shard_map/all_to_all | solution.py:534
  346.2 7.5 copy-start.42
  364.6 117.0 %copy-start.14 = (pred[16,144,256]{1,2,0:T(8,128)(4,1)S(1)}, pred[16,144,256]{1,2,0:T(8,128)(4,1)}, u32[]{:S(2)}) copy-start(pred[16,144,256]{1,2,0:T(8,128)(4,1)} %copy.201) | copy-start | bytes 1769476
  499.3 55.0 %all-to-all-start.2 = ((bf16[4,128,2048]{2,1,0:T(8,128)(2,1)}), bf16[4,128,2048]{2,1,0:T(8,128)(2,1)}, u32[]{:S(2)}, u32[]{:S(2)}) async-start(bf16[4,128,2048]{2,1,0:T(8,128)(2,1)} %convert_element_type.228), calls=%async_computation.2 | async-start | bytes 4194304 | tf_op jit(solution)/shard_map/all_to_all | solution.py:548
  505.4 15.0 %slice-start.2 = ((s8[9437184]{0:T(1024)(128)(4,1)}), s8[1048576]{0:T(1024)(128)(4,1)S(1)}, s32[]{:S(2)}) async-start(s8[9437184]{0:T(1024)(128)(4,1)} %bitcast.257), calls=%async_computation.11 | async-start | bytes 2097152
  509.4 10.9 slice-start.3
  509.4 10.9 slice-start.4
  509.4 10.9 copy-start.25
  554.4 13.8 %copy-start.2 = (bf16[16,144,2048]{2,1,0:T(8,128)(2,1)S(1)}, bf16[16,144,2048]{2,1,0:T(8,128)(2,1)}, u32[]{:S(2)}) copy-start(bf16[16,144,2048]{2,1,0:T(8,128)(2,1)} %multiply_convert_fusion) | copy-start | bytes 28311556
  574.6 265.6 %all-to-all-start.5 = ((bf16[4,128,2048]{2,1,0:T(8,128)(2,1)}), bf16[4,128,2048]{2,1,0:T(8,128)(2,1)}, u32[]{:S(2)}, u32[]{:S(2)}) async-start(bf16[4,128,2048]{2,1,0:T(8,128)(2,1)} %bitcast.283), calls=%async_computation.5 | async-start | bytes 4194304 | tf_op jit(solution)/shard_map/all_to_all | solution.py:548
  579.2 11.2 copy-start.52
  713.4 102.8 %copy-start.13 = (f32[4,32,2048]{2,1,0:T(8,128)S(1)}, f32[4,32,2048]{2,1,0:T(8,128)}, u32[]{:S(2)}) copy-start(f32[4,32,2048]{2,1,0:T(8,128)} %shard_map.266) | copy-start | bytes 3145732
  713.4 102.8 %copy-start.23 = (bf16[1,128,2048]{2,1,0:T(8,128)(2,1)S(1)}, bf16[1,128,2048]{2,1,0:T(8,128)(2,1)}, u32[]{:S(2)}) copy-start(bf16[1,128,2048]{2,1,0:T(8,128)(2,1)} %param.24) | copy-start | bytes 1572868
  819.8 7.4 copy-start.27
  819.8 7.4 copy-start.30
  833.9 12.4 %copy-start.39 = (f32[2048]{0:T(1024)S(1)}, f32[2048]{0:T(1024)}, u32[]{:S(2)}) copy-start(f32[2048]{0:T(1024)} %param.33) | copy-start | bytes 24580
  833.9 12.4 %copy-start.44 = (f32[128]{0:T(128)S(1)}, f32[128]{0:T(128)}, u32[]{:S(2)}) copy-start(f32[128]{0:T(128)} %copy-done.43) | copy-start | bytes 1540
  840.1 19.3 %slice-start.8 = ((s8[9437184]{0:T(1024)(128)(4,1)}), s8[1048576]{0:T(1024)(128)(4,1)S(1)}, s32[]{:S(2)}) async-start(s8[9437184]{0:T(1024)(128)(4,1)} %bitcast.263), calls=%async_computation.17 | async-start | bytes 2097152
  840.1 52.0 %all-to-all-start.3 = ((bf16[8,256,512]{2,1,0:T(8,128)(2,1)}), bf16[8,256,512]{2,1,0:T(8,128)(2,1)}, u32[]{:S(2)}, u32[]{:S(2)}) async-start(bf16[8,256,512]{2,1,0:T(8,128)(2,1)} %bitcast.288), calls=%async_computation.3 | async-start | bytes 4194304 | tf_op jit(solution)/shard_map/all_to_all | solution.py:539
  848.5 10.9 slice-start.9
  851.9 7.5 slice-start.10
  851.9 7.5 copy-start.54
  892.2 237.7 %all-to-all-start.4 = ((bf16[8,256,512]{2,1,0:T(8,128)(2,1)}), bf16[8,256,512]{2,1,0:T(8,128)(2,1)S(1)}, u32[]{:S(2)}, u32[]{:S(2)}) async-start(bf16[8,256,512]{2,1,0:T(8,128)(2,1)} %bitcast.282), calls=%async_computation.4 | async-start | bytes 4194304 | tf_op jit(solution)/shard_map/all_to_all | solution.py:539
  895.8 208.1 %reduce-scatter.4.cloned.1.call-start = ((), (), s32[]{:S(2)}) async-start(), calls=%async_computation.8 | async-start | bytes 1081344
  901.5 6.8 copy-start.24
  901.5 6.8 copy-start.29
  901.5 6.8 copy-start.41
  908.3 7.8 copy-start.26
  (26 other events, 96.7 us)
Sparse Core Ops, SparseCore 0:
  10.9 182.8 all-gather.1
  921.1 139.7 reduce-scatter.3
